TPU v7x, 256 devices: a whole 4x4x8 slice. The times are simulated.
256 devices in a mesh: mode: 4 (over z_lo), space: 64 (over x, y, z_hi, core).
Axes of the slice: x: 4, y: 4, z: 8 (z_hi: 2, z_lo: 4; z = z_hi * 4 + z_lo), core: 2. Of those that a mesh axis runs over, the one named last changes fastest.
Arguments:
- traces: float32 [120, 196608], P('mode', 'space'), may hold values from -6 to 6
- elem_mats: float32 [5, 36, 65536], P(None, None, 'space'), may hold values from -1.8 to 1.8
- face_links: int32 [6, 65536], P(None, 'space'), may hold values from 0 to 4095
- pair_modes: int32 [2, 1440], replicated, may hold values from 0 to 119
- pair_terms: int32 [1440], replicated, may hold values from 0 to 3
- pair_values: float32 [1440], replicated, may hold values from -3 to 3
Outputs:
- applied: float32 [120, 196608], P('mode', 'space')
Inputs may be any that keep to these rules, and one draw needn't show every extreme that they name: `face_links`: indices into an element's subdomain's 3072 faces preceded and followed by 512 faces of the neighbouring subdomains.
All inputs are finite; a program needn't handle non-finite values.
Results may differ from a plain program's by a relative error of at most 0.0001.
Values sent between devices are 32-bit elements; how exact they have to be, the bound alone decides.
No kernel may reach another device: no remote copies, remote signals or barrier semaphores. Data moves between devices by JAX's collectives and lax.ppermute only.
A program may use at most 128 MiB of HBM per device.

v0:
```python
import jax
import jax.numpy as jnp
from jax import lax
from jax.sharding import PartitionSpec as P

HALO = 512


def from_behind(block, axis, distance):
    devices = range(lax.axis_size(axis))
    route = [(i - distance, i) for i in devices if i - distance in devices]
    return lax.ppermute(block, axis, route)


def padded(array, sides, width):
    for axis, dim in sides:
        peers, length = (lax.axis_size(axis), array.shape[dim])
        up = [(i, (i + 1) % peers) for i in range(peers - 1)]
        down = [(j, i) for i, j in up]
        last = lax.slice_in_dim(array, length - width, length, axis=dim)
        first = lax.slice_in_dim(array, 0, width, axis=dim)
        before = lax.ppermute(last, axis, up)
        after = lax.ppermute(first, axis, down)
        array = jnp.concatenate([before, array, after], axis=dim)
    return array


def coupling_table(pair_modes, pair_terms, pair_values, mode_count, term_count):
    mode_ids = jnp.arange(mode_count, dtype=jnp.int32)
    row_hits = (pair_modes[0][:, None] == mode_ids[None, :]).astype(jnp.float32)
    col_hits = (pair_modes[1][:, None] == mode_ids[None, :]).astype(jnp.float32)
    tables = [jnp.eye(mode_count, dtype=jnp.float32)]
    for term in range(term_count):
        weights = jnp.where(pair_terms == term, pair_values, 0.0)
        tables.append(
            lax.dot_general(
                row_hits * weights[:, None],
                col_hits,
                (((0,), (0,)), ((), ())),
                precision=lax.Precision.HIGHEST,
            )
        )
    return jnp.stack(tables, axis=0)


def slot_table(links_row, ext_width):
    face_ids = jnp.arange(ext_width, dtype=jnp.int32)
    return (links_row[:, None] == face_ids[None, :]).astype(jnp.float32)


def gather_slots(values, links, ext_width):
    columns = []
    for slot in range(6):
        table = slot_table(links[slot], ext_width)
        columns.append(
            lax.dot_general(
                values, table, (((1,), (1,)), ((), ())), precision=lax.Precision.HIGHEST
            )
        )
    return jnp.stack(columns, axis=1)


def element_terms(values, links, mats, ext_width):
    gathered = gather_slots(values, links, ext_width)
    square_mats = mats.reshape(mats.shape[0], 6, 6, mats.shape[-1])
    running = square_mats[:, None, :, 0, :] * gathered[None, :, 0, None, :]
    for column in range(1, 6):
        running = running + square_mats[:, None, :, column, :] * gathered[None, :, column, None, :]
    return running


def assemble(local_terms, links, ext_width):
    lead = local_terms.shape[:-2]
    elem_count = local_terms.shape[-1]
    flat = local_terms.reshape((-1, 6, elem_count))
    total = jnp.zeros((flat.shape[0], ext_width), jnp.float32)
    for slot in range(6):
        table = slot_table(links[slot], ext_width)
        total = total + jnp.dot(flat[:, slot, :], table, precision=lax.Precision.HIGHEST)
    return total.reshape(lead + (ext_width,))


def fold_rims(assembled, face_count):
    left_rim = assembled[..., :HALO]
    right_rim = assembled[..., HALO + face_count :]
    middle = assembled[..., HALO : HALO + face_count]
    from_next = from_behind(left_rim, "space", -1)
    from_prev = from_behind(right_rim, "space", 1)
    return jnp.concatenate(
        [
            middle[..., :HALO] + from_prev,
            middle[..., HALO : face_count - HALO],
            middle[..., face_count - HALO :] + from_next,
        ],
        axis=-1,
    )


def body(traces, elem_mats, face_links, pair_modes, pair_terms, pair_values):
    mode_dev, face_count = traces.shape
    term_count = elem_mats.shape[0] - 1
    groups = lax.axis_size("mode")
    coupling = coupling_table(pair_modes, pair_terms, pair_values, mode_dev * groups, term_count)
    extended = padded(traces, (("space", 1),), HALO)
    ext_width = extended.shape[1]
    local_terms = element_terms(extended, face_links, elem_mats, ext_width)
    folded = fold_rims(assemble(local_terms, face_links, ext_width), face_count)
    spread_terms = folded[1:].reshape(term_count, mode_dev, groups, face_count // groups)
    mixed_modes = jnp.einsum(
        "kij,kjgn->ign",
        coupling[1:],
        lax.all_to_all(spread_terms, "mode", split_axis=2, concat_axis=1, tiled=True),
        precision=lax.Precision.HIGHEST,
    )
    coupled = lax.all_to_all(mixed_modes, "mode", split_axis=0, concat_axis=1, tiled=True)
    return folded[0] + coupled.reshape(mode_dev, face_count)


def solution(mesh):
    return jax.shard_map(
        body,
        mesh=mesh,
        in_specs=(P("mode", "space"), P(None, None, "space"), P(None, "space"), P(), P(), P()),
        out_specs=P("mode", "space"),
        check_vma=False,
    )
```

profile of v0, /device:TPU:7, one launch (start us, length us, event | category | flops | bytes accessed | tf_op | source)
XLA Modules:
  0.0 259.2 jit_solution(1444968563399989270)
XLA Ops:
  0.9 9.4 %collective-permute-start = (f32[30,512]{1,0:T(8,128)S(1)}, f32[30,512]{1,0:T(8,128)S(1)}, u32[]{:S(2)}, u32[]{:S(2)}) collective-permute-start(f32[30,512]{1,0:T(8,128)S(1)} %get-tuple-element.16), channel_id=1, source_target_pairs={{0,1},{1,2},{2,3},{3,4},{4,5},{5,6},{6,7},{7,8},{8,9},{9,10},{10,1... | collective-permute-start | bytes 184328 | tf_op jit(solution)/shard_map/ppermute | solution.py:22
  23.9 4.9 %mul.194 = f32[150,6,1024]{2,0,1:T(8,128)} reshape(f32[5,30,6,1024]{3,1,0,2:T(8,128)} %mul.193) | data formatting | bytes 7372800 | tf_op jit(solution)/shard_map/mul | solution.py:68
  31.2 4.9 %mul.187 = f32[150,6,1024]{2,0,1:T(8,128)} reshape(f32[5,30,6,1024]{3,1,0,2:T(8,128)} %mul.186) | data formatting | bytes 7372800 | tf_op jit(solution)/shard_map/mul | solution.py:68
  38.4 4.9 %mul.180 = f32[150,6,1024]{2,0,1:T(8,128)} reshape(f32[5,30,6,1024]{3,1,0,2:T(8,128)} %mul.179) | data formatting | bytes 7372800 | tf_op jit(solution)/shard_map/mul | solution.py:68
  45.7 5.0 %mul.173 = f32[150,6,1024]{2,0,1:T(8,128)} reshape(f32[5,30,6,1024]{3,1,0,2:T(8,128)} %mul.172) | data formatting | bytes 7372800 | tf_op jit(solution)/shard_map/mul | solution.py:68
  53.0 5.2 %mul.166 = f32[150,6,1024]{2,0,1:T(8,128)} reshape(f32[5,30,6,1024]{3,1,0,2:T(8,128)} %mul.165) | data formatting | bytes 7372800 | tf_op jit(solution)/shard_map/mul | solution.py:66
  58.4 8.3 %fusion.1 = f32[30,1024]{1,0:T(8,128)S(1)} fusion(f32[30,4096]{1,0:T(8,128)S(1)} %constant_dynamic-update-slice_fusion, s32[1024]{0:T(1024)S(1)} %bitcast.99), kind=kOutput, calls=%fused_computation.2 | convolution fusion | flops 1514143744 | bytes 618496 | tf_op jit(solution)/shard_map/dot_general | solution.py:56
  66.8 8.7 %fusion.3 = f32[30,1024]{1,0:T(8,128)S(1)} fusion(f32[30,4096]{1,0:T(8,128)S(1)} %constant_dynamic-update-slice_fusion, s32[1024]{0:T(1024)S(1)} %bitcast.97), kind=kOutput, calls=%fused_computation.5 | convolution fusion | flops 1514143744 | bytes 618496 | tf_op jit(solution)/shard_map/dot_general | solution.py:56
  75.6 8.3 %fusion.5 = f32[30,1024]{1,0:T(8,128)S(1)} fusion(f32[30,4096]{1,0:T(8,128)S(1)} %constant_dynamic-update-slice_fusion, s32[1024]{0:T(1024)S(1)} %bitcast.95), kind=kOutput, calls=%fused_computation.8 | convolution fusion | flops 1514143744 | bytes 618496 | tf_op jit(solution)/shard_map/dot_general | solution.py:56
  84.1 8.5 %fusion.7 = f32[30,1024]{1,0:T(8,128)S(1)} fusion(f32[30,4096]{1,0:T(8,128)S(1)} %constant_dynamic-update-slice_fusion, s32[1024]{0:T(1024)S(1)} %bitcast.93), kind=kOutput, calls=%fused_computation.11 | convolution fusion | flops 1514143744 | bytes 618496 | tf_op jit(solution)/shard_map/dot_general | solution.py:56
  92.7 9.3 %fusion.9 = f32[30,1024]{1,0:T(8,128)S(1)} fusion(f32[30,4096]{1,0:T(8,128)} %copy-done.4, s32[1024]{0:T(1024)S(1)} %bitcast.91), kind=kOutput, calls=%fused_computation.14 | convolution fusion | flops 1514143744 | bytes 618496 | tf_op jit(solution)/shard_map/dot_general | solution.py:56
  103.0 9.7 %fusion.11 = f32[30,1024]{1,0:T(8,128)S(1)} fusion(f32[30,4096]{1,0:T(8,128)} %copy-done.4, s32[1024]{0:T(1024)S(1)} %bitcast.89), kind=kOutput, calls=%fused_computation.17 | convolution fusion | flops 1514143744 | bytes 618496 | tf_op jit(solution)/shard_map/dot_general | solution.py:56
  113.7 9.4 %multiply_add_fusion = f32[150,6,1024]{2,0,1:T(8,128)S(1)} fusion(f32[150,6,1024]{2,0,1:T(8,128)} %mul.201, f32[150,6,1024]{2,0,1:T(8,128)} %mul.194, f32[150,6,1024]{2,0,1:T(8,128)} %mul.187, f32[150,6,1024]{2,0,1:T(8,128)} %mul.180, f32[150,6,1024]{2,0,1:T(8,128)} %mul.173, f32[150,6,1024]{2,0,1:T(8,128)} %mul.166, f32[150,1024]{1,0:T(8,128)S(1)} %mul.203, ...), kind=kLoop, calls=%fused_computation.35 | loop fusion | flops 10137600 | bytes 29491200 | tf_op jit(solution)/shard_map/add | solution.py:68
  123.1 6.4 %fusion = f32[150,4096]{1,0:T(8,128)S(1)} fusion(s32[1024]{0:T(1024)S(1)} %bitcast.100, f32[150,6,1024]{2,0,1:T(8,128)S(1)} %multiply_add_fusion), kind=kOutput, calls=%fused_computation.1 | convolution fusion | flops 7553941504 | bytes 3084288 | tf_op jit(solution)/shard_map/dot_general | solution.py:79
  129.5 6.6 %fusion.2 = f32[150,4096]{1,0:T(8,128)S(1)} fusion(s32[1024]{0:T(1024)S(1)} %bitcast.98, f32[150,6,1024]{2,0,1:T(8,128)S(1)} %multiply_add_fusion), kind=kOutput, calls=%fused_computation.4 | convolution fusion | flops 7553941504 | bytes 3084288 | tf_op jit(solution)/shard_map/dot_general | solution.py:79
  136.1 6.4 %fusion.4 = f32[150,4096]{1,0:T(8,128)S(1)} fusion(s32[1024]{0:T(1024)S(1)} %bitcast.96, f32[150,6,1024]{2,0,1:T(8,128)S(1)} %multiply_add_fusion), kind=kOutput, calls=%fused_computation.7 | convolution fusion | flops 7553941504 | bytes 3084288 | tf_op jit(solution)/shard_map/dot_general | solution.py:79
  142.6 6.7 %fusion.6 = f32[150,4096]{1,0:T(8,128)S(1)} fusion(s32[1024]{0:T(1024)S(1)} %bitcast.94, f32[150,6,1024]{2,0,1:T(8,128)S(1)} %multiply_add_fusion), kind=kOutput, calls=%fused_computation.10 | convolution fusion | flops 7553941504 | bytes 3084288 | tf_op jit(solution)/shard_map/dot_general | solution.py:79
  149.3 6.5 %fusion.8 = f32[150,4096]{1,0:T(8,128)S(1)} fusion(s32[1024]{0:T(1024)S(1)} %bitcast.92, f32[150,6,1024]{2,0,1:T(8,128)S(1)} %multiply_add_fusion), kind=kOutput, calls=%fused_computation.13 | convolution fusion | flops 7553941504 | bytes 3084288 | tf_op jit(solution)/shard_map/dot_general | solution.py:79
  155.8 9.0 %fusion.28 = f32[150,4096]{1,0:T(8,128)} fusion(f32[150,4096]{1,0:T(8,128)S(1)} %fusion, f32[150,4096]{1,0:T(8,128)S(1)} %fusion.2, f32[150,4096]{1,0:T(8,128)S(1)} %fusion.4, f32[150,4096]{1,0:T(8,128)S(1)} %fusion.6, f32[150,4096]{1,0:T(8,128)S(1)} %fusion.8, s32[1024]{0:T(1024)S(1)} %bitcast.90, f32[150,6,1024]{2,0,1:T(8,128)S(1)} %multiply_add_fusion), kind=kOutput, calls=%fused_computation.34 | convolution fusion | flops 7557013504 | bytes 15536128 | tf_op jit(solution)/shard_map/dot_general | solution.py:79
  166.7 7.6 %collective-permute-start.2 = (f32[5,30,512]{2,1,0:T(8,128)S(1)}, f32[5,30,512]{2,1,0:T(8,128)S(1)}, u32[]{:S(2)}, u32[]{:S(2)}) collective-permute-start(f32[5,30,512]{2,1,0:T(8,128)S(1)} %slice.139), channel_id=1, source_target_pairs={{0,1},{1,2},{2,3},{3,4},{4,5},{5,6},{6,7},{7,8},{8,9},{9,10},{10,1... | collective-permute-start | bytes 921608 | tf_op jit(solution)/shard_map/ppermute | solution.py:12
  178.4 9.2 %collective-permute-start.3 = (f32[5,30,512]{2,1,0:T(8,128)S(1)}, f32[5,30,512]{2,1,0:T(8,128)S(1)}, u32[]{:S(2)}, u32[]{:S(2)}) collective-permute-start(f32[5,30,512]{2,1,0:T(8,128)S(1)} %get-tuple-element.8), channel_id=1, source_target_pairs={{1,0},{2,1},{3,2},{4,3},{5,4},{6,5},{7,6},{8,7},{9,8},{10,9},{11,1... | collective-permute-start | bytes 921608 | tf_op jit(solution)/shard_map/ppermute | solution.py:12
  197.8 9.7 %all-to-all-start = ((f32[4,30,4,768]{3,0,1,2:T(4,128)}), f32[4,30,4,768]{3,0,1,2:T(4,128)S(1)}, u32[]{:S(2)}, u32[]{:S(2)}) async-start(f32[4,30,4,768]{3,0,1,2:T(4,128)} %copy.28), calls=%async_computation | async-start | bytes 2949120 | tf_op jit(solution)/shard_map/all_to_all | solution.py:112
  215.1 26.2 %all-to-all-done = f32[4,30,4,768]{3,0,1,2:T(4,128)S(1)} async-done(((f32[4,30,4,768]{3,0,1,2:T(4,128)}), f32[4,30,4,768]{3,0,1,2:T(4,128)S(1)}, u32[]{:S(2)}, u32[]{:S(2)}) %all-to-all-start) | async-done | bytes 1474592 | tf_op jit(solution)/shard_map/all_to_all | solution.py:112
  243.7 14.0 %all_to_all.30 = f32[120,1,768]{2,1,0:T(1,128)S(1)} all-to-all(f32[120,1,768]{2,1,0:T(1,128)S(1)} %copy.30), channel_id=1, replica_groups=mesh['mode'=4,'space'=64] {'mode'}, dimensions={0} | all-to-all | bytes 737280 | tf_op jit(solution)/shard_map/all_to_all | solution.py:115
  (68 shorter events, 53.5 us)
Async XLA Ops:
  0.0 14.3 %copy-start.2 = (s32[6,1024]{1,0:T(8,128)S(1)}, s32[6,1024]{1,0:T(8,128)}, u32[]{:S(2)}) copy-start(s32[6,1024]{1,0:T(8,128)} %param.8) | copy-start | bytes 73732
  0.9 57.4 %collective-permute-start = (f32[30,512]{1,0:T(8,128)S(1)}, f32[30,512]{1,0:T(8,128)S(1)}, u32[]{:S(2)}, u32[]{:S(2)}) collective-permute-start(f32[30,512]{1,0:T(8,128)S(1)} %get-tuple-element.16), channel_id=1, source_target_pairs={{0,1},{1,2},{2,3},{3,4},{4,5},{5,6},{6,7},{7,8},{8,9},{9,10},{10,1... | collective-permute-start | bytes 184328 | tf_op jit(solution)/shard_map/ppermute | solution.py:22
  10.3 48.0 %collective-permute-start.1 = (f32[30,512]{1,0:T(8,128)S(1)}, f32[30,512]{1,0:T(8,128)S(1)}, u32[]{:S(2)}, u32[]{:S(2)}) collective-permute-start(f32[30,512]{1,0:T(8,128)S(1)} %get-tuple-element.15), channel_id=1, source_target_pairs={{1,0},{2,1},{3,2},{4,3},{5,4},{6,5},{7,6},{8,7},{9,8},{10,9},{11,1... | collective-permute-start | bytes 184328 | tf_op jit(solution)/shard_map/ppermute | solution.py:23
  53.0 5.3 %copy-start.1 = (f32[30,3072]{1,0:T(8,128)S(1)}, f32[30,3072]{1,0:T(8,128)}, u32[]{:S(2)}) copy-start(f32[30,3072]{1,0:T(8,128)} %param.6) | copy-start | bytes 1105924
  58.3 25.7 %copy-start.4 = (f32[30,4096]{1,0:T(8,128)}, f32[30,4096]{1,0:T(8,128)S(1)}, u32[]{:S(2)}) copy-start(f32[30,4096]{1,0:T(8,128)S(1)} %constant_dynamic-update-slice_fusion) | copy-start | bytes 1474564
  166.7 11.8 %copy-start = (f32[5,30,4096]{2,1,0:T(8,128)}, f32[5,30,4096]{2,1,0:T(8,128)S(1)}, u32[]{:S(2)}) copy-start(f32[5,30,4096]{2,1,0:T(8,128)S(1)} %reshape.56) | copy-start | bytes 7372804
  166.7 11.7 %collective-permute-start.2 = (f32[5,30,512]{2,1,0:T(8,128)S(1)}, f32[5,30,512]{2,1,0:T(8,128)S(1)}, u32[]{:S(2)}, u32[]{:S(2)}) collective-permute-start(f32[5,30,512]{2,1,0:T(8,128)S(1)} %slice.139), channel_id=1, source_target_pairs={{0,1},{1,2},{2,3},{3,4},{4,5},{5,6},{6,7},{7,8},{8,9},{9,10},{10,1... | collective-permute-start | bytes 921608 | tf_op jit(solution)/shard_map/ppermute | solution.py:12
  178.4 13.2 %collective-permute-start.3 = (f32[5,30,512]{2,1,0:T(8,128)S(1)}, f32[5,30,512]{2,1,0:T(8,128)S(1)}, u32[]{:S(2)}, u32[]{:S(2)}) collective-permute-start(f32[5,30,512]{2,1,0:T(8,128)S(1)} %get-tuple-element.8), channel_id=1, source_target_pairs={{1,0},{2,1},{3,2},{4,3},{5,4},{6,5},{7,6},{8,7},{9,8},{10,9},{11,1... | collective-permute-start | bytes 921608 | tf_op jit(solution)/shard_map/ppermute | solution.py:12
  192.8 14.7 %copy-start.3 = (s32[2,1440]{1,0:T(2,128)S(1)}, s32[2,1440]{1,0:T(2,128)}, u32[]{:S(2)}) copy-start(s32[2,1440]{1,0:T(2,128)} %param.9) | copy-start | bytes 34564
  194.7 12.8 %copy-start.5 = (f32[1440]{0:T(1024)S(1)}, f32[1440]{0:T(1024)}, u32[]{:S(2)}) copy-start(f32[1440]{0:T(1024)} %param.11) | copy-start | bytes 17284
  194.7 12.8 %copy-start.6 = (s32[1440]{0:T(1024)S(1)}, s32[1440]{0:T(1024)}, u32[]{:S(2)}) copy-start(s32[1440]{0:T(1024)} %param.10) | copy-start | bytes 17284
  197.8 43.5 %all-to-all-start = ((f32[4,30,4,768]{3,0,1,2:T(4,128)}), f32[4,30,4,768]{3,0,1,2:T(4,128)S(1)}, u32[]{:S(2)}, u32[]{:S(2)}) async-start(f32[4,30,4,768]{3,0,1,2:T(4,128)} %copy.28), calls=%async_computation | async-start | bytes 2949120 | tf_op jit(solution)/shard_map/all_to_all | solution.py:112
where the time goes:
time: 264 us; the launch traced here: 259 us
  matrix products  104 us (39%)
  local copies, waits for them, and re-layouts  58.3 us (22%)
  starting transfers between devices  37.7 us (14%)
  waiting for transfers between devices  32.9 us (12%)
  blocking collectives  14 us (5%)
  other arithmetic  11.4 us (4%)
    dot_general x6, matrix products, gather_slots(): lax.dot_general(values, table, (((1,), (1,)), ((), ())), precision=lax.Pr...  52.8 us
    dot_general x6, matrix products, assemble(): jnp.dot(flat[:, slot, :], table, precision=lax.Precision.HIGHEST)  41.7 us
    mul x23, local copies, waits for them, and re-layouts, element_terms(): square_mats[:, None, :, column, :] * gathered[None, :, column, None, :]  38.1 us
    all_to_all x1, waiting for transfers between devices, body(): lax.all_to_all(spread_terms, 'mode', split_axis=2, concat_axis=1, tiled=T...  26.2 us
    ppermute x2, starting transfers between devices, from_behind(): return lax.ppermute(block, axis, route)  16.8 us
    all_to_all x1, blocking collectives, body(): lax.all_to_all(mixed_modes, 'mode', split_axis=0, concat_axis=1, tiled=True)  14 us
    all_to_all x1, starting transfers between devices, body(): lax.all_to_all(spread_terms, 'mode', split_axis=2, concat_axis=1, tiled=T...  9.69 us
    ppermute x1, starting transfers between devices, padded(): before = lax.ppermute(last, axis, up)  9.38 us
  transfers between devices with their start and end apart: 5, of which 3 were waited for; matrix products, arithmetic and copies ran while one was open for 21% of the time, Pallas kernels for 0%

commit v1 on v0

v1 whole, which is shorter than its diff:
```python
import jax
import jax.numpy as jnp
from jax import lax
from jax.experimental import pallas as pl
from jax.experimental.pallas import tpu as pltpu
from jax.sharding import PartitionSpec as P

HALO = 512
MD = 30
SLOTS = 6
E = 1024
OWN = 3072
TERMS = 4
LANES = SLOTS * E
NN = (((1,), (0,)), ((), ()))
NT = (((1,), (1,)), ((), ()))
F32 = jnp.float32
BF16 = jnp.bfloat16


def split_hi_lo(x):
    hi = x.astype(BF16)
    lo = (x - hi.astype(F32)).astype(BF16)
    return hi, lo


def codes(links):
    f = jnp.where(links < HALO, links + OWN, jnp.where(links < HALO + OWN, links - HALO, links))
    quad = (f >> 8) & 3
    row = ((f >> 10) << 8) | (f & 255)
    return row, quad


def table_kernel(me_ref, modes_ref, terms_ref, values_ref, out_ref):
    me = me_ref[0]
    n = values_ref.shape[1]
    i_loc = modes_ref[0:1, :] - MD * me
    row = jnp.where((i_loc >= 0) & (i_loc < MD), terms_ref[...] * 32 + i_loc, -1)
    j = modes_ref[1:2, :]
    part = (j >= MD).astype(jnp.int32) + (j >= 2 * MD).astype(jnp.int32) + (j >= 3 * MD).astype(jnp.int32)
    col = (part ^ me) * 64 + (j - MD * part)
    rid = lax.broadcasted_iota(jnp.int32, (128, n), 0)
    cid = lax.broadcasted_iota(jnp.int32, (256, n), 0)
    cols = jnp.where((cid & ~32) == col, 1.0, 0.0).astype(BF16)
    left = jnp.where(rid == row, values_ref[...], 0.0)
    a = left.astype(BF16)
    rest = left - a.astype(F32)
    b = rest.astype(BF16)
    c = (rest - b.astype(F32)).astype(BF16)
    total = lax.dot_general(a, cols, NT, preferred_element_type=F32)
    total = total + lax.dot_general(b, cols, NT, preferred_element_type=F32)
    total = total + lax.dot_general(c, cols, NT, preferred_element_type=F32)
    hi, lo = split_hi_lo(total)
    out_ref[0:128, :] = hi
    out_ref[128:256, :] = lo


def coupling_table(me, pair_modes, pair_terms, pair_values):
    n = pair_values.shape[0]
    wide = -(-n // 128) * 128
    modes = jnp.pad(pair_modes, ((0, 0), (0, wide - n)))
    terms = jnp.pad(pair_terms, (0, wide - n)).reshape(1, wide)
    values = jnp.pad(pair_values, (0, wide - n)).reshape(1, wide)
    return pl.pallas_call(
        table_kernel,
        out_shape=jax.ShapeDtypeStruct((256, 256), BF16),
        in_specs=[pl.BlockSpec(memory_space=pltpu.SMEM)] + [pl.BlockSpec(memory_space=pltpu.VMEM)] * 3,
        out_specs=pl.BlockSpec(memory_space=pltpu.VMEM),
    )(me, modes, terms, values)


def gather_kernel(x_ref, h_ref, links_ref, out_ref, t_ref):
    t_ref[...] = jnp.zeros(t_ref.shape, BF16)
    for chunk in range(4):
        for q in range(4):
            if chunk < 3:
                piece = x_ref[:, chunk * 1024 + q * 256 : chunk * 1024 + (q + 1) * 256]
            else:
                piece = h_ref[:, q * 256 : (q + 1) * 256]
            hi, lo = split_hi_lo(piece)
            t_ref[q * 64 : q * 64 + MD, chunk * 256 : (chunk + 1) * 256] = hi
            t_ref[q * 64 + 32 : q * 64 + 32 + MD, chunk * 256 : (chunk + 1) * 256] = lo
    t = t_ref[...]
    step = 512

    def one(i, carry):
        base = pl.multiple_of(i * step, step)
        row, quad = codes(links_ref[:, pl.ds(base, step)])
        rid = lax.broadcasted_iota(jnp.int32, (1024, step), 0)
        hot = jnp.where(rid == row, 1.0, 0.0).astype(BF16)
        got = lax.dot_general(t, hot, NN, preferred_element_type=F32)
        total = jnp.zeros((64, step), F32)
        for q in range(4):
            total = total + jnp.where(quad == q, got[q * 64 : (q + 1) * 64], 0.0)
        out_ref[:, pl.ds(base, step)] = total.astype(BF16)
        return carry

    lax.fori_loop(0, LANES // step, one, 0)


def gather(x, h, links):
    return pl.pallas_call(
        gather_kernel,
        out_shape=jax.ShapeDtypeStruct((64, LANES), BF16),
        in_specs=[pl.BlockSpec(memory_space=pltpu.VMEM)] * 3,
        out_specs=pl.BlockSpec(memory_space=pltpu.VMEM),
        scratch_shapes=[pltpu.VMEM((256, 1024), BF16)],
    )(x, h, links)


def scatter_chunk(l_ref, links_ref, chunk):
    total = jnp.zeros((256, 256), F32)
    for a in range(SLOTS):
        row, _ = codes(links_ref[:, a * E : (a + 1) * E])
        rid = lax.broadcasted_iota(jnp.int32, (256, E), 0) + chunk * 256
        hot = jnp.where(rid == row, 1.0, 0.0).astype(BF16)
        total = total + lax.dot_general(l_ref[:, a * E : (a + 1) * E], hot, NT, preferred_element_type=F32)
    return total


def element_kernel(g0, g1, g2, g3, table_ref, mats_ref, links_ref, l_ref, rims_ref, y_ref):
    step = 256

    def one(i, carry):
        base = pl.multiple_of(i * step, step)
        for b in range(SLOTS):
            here = pl.ds(b * E + base, step)
            right = jnp.concatenate([g[:, here] for g in (g0, g1, g2, g3)], axis=0)
            got = lax.dot_general(table_ref[...], right, NN, preferred_element_type=F32)
            own = g0[:, here].astype(F32)
            y_ref[b, 0:32] = own[0:32] + own[32:64]
            y_ref[b, 32:160] = got[0:128] + got[128:256]
        for a in range(SLOTS):
            acc = None
            for b in range(SLOTS):
                for k in range(TERMS + 1):
                    m = mats_ref[k, 6 * a + b : 6 * a + b + 1, pl.ds(base, step)]
                    term = m * y_ref[b, 32 * k : 32 * (k + 1)]
                    acc = term if acc is None else acc + term
            here = pl.ds(a * E + base, step)
            _, quad = codes(links_ref[:, here])
            hi = acc.astype(BF16).astype(F32)
            lo = acc - hi
            for q in range(4):
                l_ref[q * 64 : q * 64 + 32, here] = jnp.where(quad == q, hi, 0.0).astype(BF16)
                l_ref[q * 64 + 32 : q * 64 + 64, here] = jnp.where(quad == q, lo, 0.0).astype(BF16)
        return carry

    lax.fori_loop(0, E // step, one, 0)
    total = scatter_chunk(l_ref, links_ref, 3)
    for q in range(4):
        both = total[q * 64 : q * 64 + 32] + total[q * 64 + 32 : q * 64 + 64]
        rims_ref[:, q * 256 : (q + 1) * 256] = both[0:MD]


def elements(gs, table, mats, links):
    return pl.pallas_call(
        element_kernel,
        out_shape=(jax.ShapeDtypeStruct((256, LANES), BF16), jax.ShapeDtypeStruct((MD, 2 * HALO), F32)),
        in_specs=[pl.BlockSpec(memory_space=pltpu.VMEM)] * 7,
        out_specs=(pl.BlockSpec(memory_space=pltpu.VMEM),) * 2,
        scratch_shapes=[pltpu.VMEM((SLOTS, 160, 256), F32)],
    )(*gs, table, mats, links)


def own_kernel(l_ref, links_ref, out_ref):
    for chunk in range(3):
        total = scatter_chunk(l_ref, links_ref, chunk)
        for q in range(4):
            both = total[q * 64 : q * 64 + 32] + total[q * 64 + 32 : q * 64 + 64]
            out_ref[:, chunk * 1024 + q * 256 : chunk * 1024 + (q + 1) * 256] = both[0:MD]


def scatter_own(l, links):
    return pl.pallas_call(
        own_kernel,
        out_shape=jax.ShapeDtypeStruct((MD, OWN), F32),
        in_specs=[pl.BlockSpec(memory_space=pltpu.VMEM)] * 2,
        out_specs=pl.BlockSpec(memory_space=pltpu.VMEM),
    )(l, links)


def body(traces, elem_mats, face_links, pair_modes, pair_terms, pair_values):
    parts = lax.axis_size("space")
    me = lax.axis_index("mode").astype(jnp.int32).reshape(1)
    up = [(i, i + 1) for i in range(parts - 1)]
    down = [(i + 1, i) for i in range(parts - 1)]
    xor = lambda d: [(i, i ^ d) for i in range(4)]
    others = {d: lax.ppermute(traces, "mode", xor(d)) for d in (2, 1, 3)}
    left = lax.ppermute(traces[:, OWN - HALO :], "space", up)
    right = lax.ppermute(traces[:, :HALO], "space", down)
    halo = jnp.concatenate([left, right], axis=1)
    halos = {d: lax.ppermute(halo, "mode", xor(d)) for d in (2, 1, 3)}
    links = face_links.reshape(1, LANES)
    table = coupling_table(me, pair_modes, pair_terms, pair_values)
    gs = [gather(traces, halo, links)] + [gather(others[d], halos[d], links) for d in (1, 2, 3)]
    local, rims = elements(gs, table, elem_mats, links)
    own = scatter_own(local, links)
    from_next = lax.ppermute(rims[:, :HALO], "space", down)
    from_prev = lax.ppermute(rims[:, HALO:], "space", up)
    return jnp.concatenate(
        [own[:, :HALO] + from_prev, own[:, HALO : OWN - HALO], own[:, OWN - HALO :] + from_next], axis=1
    )


def solution(mesh):
    return jax.shard_map(
        body,
        mesh=mesh,
        in_specs=(P("mode", "space"), P(None, None, "space"), P(None, "space"), P(), P(), P()),
        out_specs=P("mode", "space"),
        check_vma=False,
    )
```

time: 264 us -> 121 us (0.46); the launches traced: 259 us -> 119 us
  matrix products: 104 us -> 0 us
  local copies, waits for them, and re-layouts: 58.3 us -> 11.6 us
  Pallas kernels: 0 us -> 45.2 us
  blocking collectives: 14 us -> 0 us
  starting transfers between devices: 37.7 us -> 25.3 us
  other arithmetic: 11.4 us -> 1.66 us
    dot_general x17 -> x0, matrix products: 104 us -> none  [the longest x6 52.8 us: gather_slots(): lax.dot_general(values, table, (((1,), (1,)), ((), ())), precision=lax.Pr...]
    mul x27 -> x0, local copies, waits for them, and re-layouts: 46.7 us -> none  [the longest x23 38.1 us: element_terms(): square_mats[:, None, :, column, :] * gathered[None, :, column, None, :]]
    pallas_call x0 -> x7, Pallas kernels: none -> 45.2 us  [the longest x4 30.3 us: gather(): pl.pallas_call(gather_kernel, out_shape=jax.ShapeDtypeStruct((64, LANES),...]
    ppermute x4 -> x10, waiting for transfers between devices: 6.67 us -> 35.4 us  [the longest x1 26 us: body(): right = lax.ppermute(traces[:, :HALO], 'space', down)]
    all_to_all x1 -> x0, waiting for transfers between devices: 26.2 us -> none  [body(): lax.all_to_all(spread_terms, 'mode', split_axis=2, concat_axis=1, tiled=T...]
    all_to_all x1 -> x0, blocking collectives: 14 us -> none  [body(): lax.all_to_all(mixed_modes, 'mode', split_axis=0, concat_axis=1, tiled=True)]
    add x4 -> x1, other arithmetic: 11.2 us -> 0.89 us  [body(): own[:, :HALO] + from_prev]
    all_to_all x1 -> x0, starting transfers between devices: 9.69 us -> none  [body(): lax.all_to_all(spread_terms, 'mode', split_axis=2, concat_axis=1, tiled=T...]
  transfers between devices with their start and end apart: 5 -> 10, of which waited for: 3 -> 3; matrix products, arithmetic and copies ran while one was open for 21% -> 5% of each run, Pallas kernels for 0% -> 25%
where the time goes in v1:
time: 121 us; the launch traced here: 119 us
  Pallas kernels  45.2 us (37%)
  waiting for transfers between devices  35.4 us (29%)
  starting transfers between devices  25.3 us (21%)
  local copies, waits for them, and re-layouts  11.6 us (10%)
  other arithmetic  1.66 us (1%)
    pallas_call x4, Pallas kernels, gather(): pl.pallas_call(gather_kernel, out_shape=jax.ShapeDtypeStruct((64, LANES),...  30.3 us
    ppermute x1, waiting for transfers between devices, body(): right = lax.ppermute(traces[:, :HALO], 'space', down)  26 us
    ppermute x1, starting transfers between devices, body(): left = lax.ppermute(traces[:, OWN - HALO:], 'space', up)  9.38 us
    ppermute x1, starting transfers between devices, body(): from_prev = lax.ppermute(rims[:, HALO:], 'space', up)  8.05 us
    ppermute x3, waiting for transfers between devices, body(): halos = {d: lax.ppermute(halo, 'mode', xor(d)) for d in (2, 1, 3)}  7.88 us
    pallas_call x1, Pallas kernels, elements(): pl.pallas_call(element_kernel, out_shape=(jax.ShapeDtypeStruct((256, LANE...  7.28 us
    pallas_call x1, Pallas kernels, scatter_own(): pl.pallas_call(own_kernel, out_shape=jax.ShapeDtypeStruct((MD, OWN), F32)...  5.28 us
    unnamed x16, local copies, waits for them, and re-layouts  4.95 us
  transfers between devices with their start and end apart: 10, of which 3 were waited for; matrix products, arithmetic and copies ran while one was open for 5% of the time, Pallas kernels for 25%

profile of v1, /device:TPU:7, one launch (start us, length us, event | category | flops | bytes accessed | tf_op | source)
XLA Modules:
  0.0 119.3 jit_solution(6746313676777855034)
XLA Ops:
  0.0 0.9 fusion
  0.9 9.4 %collective-permute-start = (f32[30,512]{1,0:T(8,128)S(1)}, f32[30,512]{1,0:T(8,128)S(1)}, u32[]{:S(2)}, u32[]{:S(2)}) collective-permute-start(f32[30,512]{1,0:T(8,128)S(1)} %get-tuple-element.12), channel_id=1, source_target_pairs={{0,1},{1,2},{2,3},{3,4},{4,5},{5,6},{6,7},{7,8},{8,9},{9,10},{10,1... | collective-permute-start | bytes 184328 | tf_op jit(solution)/shard_map/ppermute | solution.py:190
  10.3 0.8 collective-permute-start.2
  11.1 1.6 %collective-permute-start.6 = (f32[30,3072]{1,0:T(8,128)}, f32[30,3072]{1,0:T(8,128)S(1)}, u32[]{:S(2)}, u32[]{:S(2)}) collective-permute-start(f32[30,3072]{1,0:T(8,128)} %x_ref.1), channel_id=1, source_target_pairs={{0,192},{64,128},{128,64},{192,0},{1,193},{65,129},{129,65},{193,1... | collective-permute-start | bytes 1105928 | tf_op jit(solution)/shard_map/ppermute | solution.py:189
  13.0 1.9 %collective-permute-start.1 = (f32[30,512]{1,0:T(8,128)S(1)}, f32[30,512]{1,0:T(8,128)S(1)}, u32[]{:S(2)}, u32[]{:S(2)}) collective-permute-start(f32[30,512]{1,0:T(8,128)S(1)} %get-tuple-element.11), channel_id=1, source_target_pairs={{1,0},{2,1},{3,2},{4,3},{5,4},{6,5},{7,6},{8,7},{9,8},{10,9},{11,1... | collective-permute-start | bytes 184328 | tf_op jit(solution)/shard_map/ppermute | solution.py:191
  14.9 26.0 %collective-permute-done.1 = f32[30,512]{1,0:T(8,128)S(1)} collective-permute-done((f32[30,512]{1,0:T(8,128)S(1)}, f32[30,512]{1,0:T(8,128)S(1)}, u32[]{:S(2)}, u32[]{:S(2)}) %collective-permute-start.1) | collective-permute-done | bytes 61472 | tf_op jit(solution)/shard_map/ppermute | solution.py:191
  41.1 1.2 %collective-permute-start.7 = (f32[30,1024]{1,0:T(8,128)S(1)}, f32[30,1024]{1,0:T(8,128)S(1)}, u32[]{:S(2)}, u32[]{:S(2)}) collective-permute-start(f32[30,1024]{1,0:T(8,128)S(1)} %constant_dynamic-update-slice_fusion.h_ref), channel_id=1, source_target_pairs={{0,192},{64,128},{128,64},{192,0},{1,193},{65,129},{129,65},{193,1... | collective-permute-start | bytes 368648 | tf_op jit(solution)/shard_map/ppermute | solution.py:193
  42.3 7.9 %collective-permute-done.3.h_ref = f32[30,1024]{1,0:T(8,128)S(1)} collective-permute-done((f32[30,1024]{1,0:T(8,128)S(1)}, f32[30,1024]{1,0:T(8,128)S(1)}, u32[]{:S(2)}, u32[]{:S(2)}) %collective-permute-start.3) | collective-permute-done | bytes 122912 | tf_op jit(solution)/shard_map/ppermute | solution.py:193
  52.8 1.3 %pad.12.modes_ref = s32[2,1536]{1,0:T(2,128)} pad(s32[2,1440]{1,0:T(2,128)} %param.9, s32[]{:T(128)} %constant.8.clone.1), padding=0_0x0_96 | pad | bytes 23812 | tf_op jit(solution)/shard_map/jit(_pad)/pad | solution.py:61
  54.1 1.4 %copy.7 = s32[1,1,6,1024]{3,1,2,0:T(1,128)} copy(s32[1,1,6,1024]{3,2,1,0:T(8,128)} %bitcast.10) | data formatting | bytes 49152
  55.5 2.3 %shard_map.68.table_ref = bf16[256,256]{1,0:T(8,128)(2,1)} custom-call(s32[1]{0:T(128)} %bitcast.me_ref, s32[2,1536]{1,0:T(2,128)} %pad.12.modes_ref, s32[1,1536]{1,0:T(1,128)} %reshape.14.terms_ref, f32[1,1536]{1,0:T(1,128)} %reshape.15.values_ref), custom_call_target="tpu_custom_call" | custom-call | tf_op jit(solution)/shard_map/pallas_call | solution.py:64
  57.9 7.6 %shard_map.64.g0 = bf16[64,6144]{1,0:T(8,128)(2,1)} custom-call(f32[30,3072]{1,0:T(8,128)} %x_ref.1, f32[30,1024]{1,0:T(8,128)} %copy-done.3, s32[1,6144]{1,0:T(1,128)} %bitcast.4), custom_call_target="tpu_custom_call" | custom-call | tf_op jit(solution)/shard_map/pallas_call | solution.py:102
  66.2 7.6 %shard_map.65.g1 = bf16[64,6144]{1,0:T(8,128)(2,1)} custom-call(f32[30,3072]{1,0:T(8,128)} %copy-done.2, f32[30,1024]{1,0:T(8,128)} %copy-done.6, s32[1,6144]{1,0:T(1,128)} %bitcast.5), custom_call_target="tpu_custom_call" | custom-call | tf_op jit(solution)/shard_map/pallas_call | solution.py:102
  75.2 7.6 %shard_map.67.g3 = bf16[64,6144]{1,0:T(8,128)(2,1)} custom-call(f32[30,3072]{1,0:T(8,128)} %copy-done.1, f32[30,1024]{1,0:T(8,128)} %copy-done.5, s32[1,6144]{1,0:T(1,128)} %bitcast.6), custom_call_target="tpu_custom_call" | custom-call | tf_op jit(solution)/shard_map/pallas_call | solution.py:102
  84.1 7.6 %shard_map.66.g2 = bf16[64,6144]{1,0:T(8,128)(2,1)} custom-call(f32[30,3072]{1,0:T(8,128)} %copy-done, f32[30,1024]{1,0:T(8,128)} %copy-done.4, s32[1,6144]{1,0:T(1,128)} %bitcast.7), custom_call_target="tpu_custom_call" | custom-call | tf_op jit(solution)/shard_map/pallas_call | solution.py:102
  91.7 7.3 %shard_map.69 = (bf16[256,6144]{1,0:T(8,128)(2,1)}, f32[30,1024]{1,0:T(8,128)}) custom-call(bf16[64,6144]{1,0:T(8,128)(2,1)} %shard_map.64.g0, bf16[64,6144]{1,0:T(8,128)(2,1)} %shard_map.65.g1, bf16[64,6144]{1,0:T(8,128)(2,1)} %shard_map.66.g2, bf16[64,6144]{1,0:T(8,128)(2,1)} %shard_map.67.g3, bf16[256,256]{1,0:T(8,128)(2,1)} %shard_map.68.table_ref, ...), custom_call_target="tpu_custom_call" | custom-call | tf_op jit(solution)/shard_map/pallas_call | solution.py:157
  99.0 0.9 fusion.1
  99.9 8.1 %collective-permute-start.8 = (f32[30,512]{1,0:T(8,128)S(1)}, f32[30,512]{1,0:T(8,128)S(1)}, u32[]{:S(2)}, u32[]{:S(2)}) collective-permute-start(f32[30,512]{1,0:T(8,128)S(1)} %get-tuple-element.13), channel_id=1, source_target_pairs={{0,1},{1,2},{2,3},{3,4},{4,5},{5,6},{6,7},{7,8},{8,9},{9,10},{10,1... | collective-permute-start | bytes 184328 | tf_op jit(solution)/shard_map/ppermute | solution.py:200
  107.9 1.9 %collective-permute-start.9 = (f32[30,512]{1,0:T(8,128)S(1)}, f32[30,512]{1,0:T(8,128)S(1)}, u32[]{:S(2)}, u32[]{:S(2)}) collective-permute-start(f32[30,512]{1,0:T(8,128)S(1)} %get-tuple-element.14), channel_id=1, source_target_pairs={{1,0},{2,1},{3,2},{4,3},{5,4},{6,5},{7,6},{8,7},{9,8},{10,9},{11,1... | collective-permute-start | bytes 184328 | tf_op jit(solution)/shard_map/ppermute | solution.py:199
  109.9 5.3 %shard_map.70 = f32[30,3072]{1,0:T(8,128)} custom-call(bf16[256,6144]{1,0:T(8,128)(2,1)} %get-tuple-element.7.l_ref, s32[1,6144]{1,0:T(1,128)} %bitcast.9), custom_call_target="tpu_custom_call" | custom-call | tf_op jit(solution)/shard_map/pallas_call | solution.py:175
  115.1 1.0 slice.29
  116.1 1.5 %collective-permute-done.9 = f32[30,512]{1,0:T(8,128)S(1)} collective-permute-done((f32[30,512]{1,0:T(8,128)S(1)}, f32[30,512]{1,0:T(8,128)S(1)}, u32[]{:S(2)}, u32[]{:S(2)}) %collective-permute-start.9) | collective-permute-done | bytes 61472 | tf_op jit(solution)/shard_map/ppermute | solution.py:199
  117.6 0.9 slice_add_fusion.1
  118.5 0.8 pad_maximum_fusion
  (30 shorter events, 6.6 us)
Async XLA Ops:
  0.9 14.0 %collective-permute-start = (f32[30,512]{1,0:T(8,128)S(1)}, f32[30,512]{1,0:T(8,128)S(1)}, u32[]{:S(2)}, u32[]{:S(2)}) collective-permute-start(f32[30,512]{1,0:T(8,128)S(1)} %get-tuple-element.12), channel_id=1, source_target_pairs={{0,1},{1,2},{2,3},{3,4},{4,5},{5,6},{6,7},{7,8},{8,9},{9,10},{10,1... | collective-permute-start | bytes 184328 | tf_op jit(solution)/shard_map/ppermute | solution.py:190
  10.3 55.2 %collective-permute-start.2 = (f32[30,3072]{1,0:T(8,128)}, f32[30,3072]{1,0:T(8,128)S(1)}, u32[]{:S(2)}, u32[]{:S(2)}) collective-permute-start(f32[30,3072]{1,0:T(8,128)} %x_ref.1), channel_id=1, source_target_pairs={{0,64},{64,0},{128,192},{192,128},{1,65},{65,1},{129,193},{193,129... | collective-permute-start | bytes 1105928 | tf_op jit(solution)/shard_map/ppermute | solution.py:189
  11.1 62.7 %collective-permute-start.6 = (f32[30,3072]{1,0:T(8,128)}, f32[30,3072]{1,0:T(8,128)S(1)}, u32[]{:S(2)}, u32[]{:S(2)}) collective-permute-start(f32[30,3072]{1,0:T(8,128)} %x_ref.1), channel_id=1, source_target_pairs={{0,192},{64,128},{128,64},{192,0},{1,193},{65,129},{129,65},{193,1... | collective-permute-start | bytes 1105928 | tf_op jit(solution)/shard_map/ppermute | solution.py:189
  12.7 70.0 %collective-permute-start.4 = (f32[30,3072]{1,0:T(8,128)}, f32[30,3072]{1,0:T(8,128)S(1)}, u32[]{:S(2)}, u32[]{:S(2)}) collective-permute-start(f32[30,3072]{1,0:T(8,128)} %x_ref.1), channel_id=1, source_target_pairs={{0,128},{64,192},{128,0},{192,64},{1,129},{65,193},{129,1},{193,65... | collective-permute-start | bytes 1105928 | tf_op jit(solution)/shard_map/ppermute | solution.py:189
  13.0 28.0 %collective-permute-start.1 = (f32[30,512]{1,0:T(8,128)S(1)}, f32[30,512]{1,0:T(8,128)S(1)}, u32[]{:S(2)}, u32[]{:S(2)}) collective-permute-start(f32[30,512]{1,0:T(8,128)S(1)} %get-tuple-element.11), channel_id=1, source_target_pairs={{1,0},{2,1},{3,2},{4,3},{5,4},{6,5},{7,6},{8,7},{9,8},{10,9},{11,1... | collective-permute-start | bytes 184328 | tf_op jit(solution)/shard_map/ppermute | solution.py:191
  41.0 16.9 %copy-start.3 = (f32[30,1024]{1,0:T(8,128)}, f32[30,1024]{1,0:T(8,128)S(1)}, u32[]{:S(2)}) copy-start(f32[30,1024]{1,0:T(8,128)S(1)} %constant_dynamic-update-slice_fusion.h_ref) | copy-start | bytes 368644
  41.0 9.2 %collective-permute-start.3 = (f32[30,1024]{1,0:T(8,128)S(1)}, f32[30,1024]{1,0:T(8,128)S(1)}, u32[]{:S(2)}, u32[]{:S(2)}) collective-permute-start(f32[30,1024]{1,0:T(8,128)S(1)} %constant_dynamic-update-slice_fusion.h_ref), channel_id=1, source_target_pairs={{0,64},{64,0},{128,192},{192,128},{1,65},{65,1},{129,193},{193,129... | collective-permute-start | bytes 368648 | tf_op jit(solution)/shard_map/ppermute | solution.py:193
  41.1 32.7 %collective-permute-start.7 = (f32[30,1024]{1,0:T(8,128)S(1)}, f32[30,1024]{1,0:T(8,128)S(1)}, u32[]{:S(2)}, u32[]{:S(2)}) collective-permute-start(f32[30,1024]{1,0:T(8,128)S(1)} %constant_dynamic-update-slice_fusion.h_ref), channel_id=1, source_target_pairs={{0,192},{64,128},{128,64},{192,0},{1,193},{65,129},{129,65},{193,1... | collective-permute-start | bytes 368648 | tf_op jit(solution)/shard_map/ppermute | solution.py:193
  50.2 15.3 %copy-start.6 = (f32[30,1024]{1,0:T(8,128)}, f32[30,1024]{1,0:T(8,128)S(1)}, u32[]{:S(2)}) copy-start(f32[30,1024]{1,0:T(8,128)S(1)} %collective-permute-done.3.h_ref) | copy-start | bytes 368644
  50.2 32.6 %collective-permute-start.5 = (f32[30,1024]{1,0:T(8,128)S(1)}, f32[30,1024]{1,0:T(8,128)S(1)}, u32[]{:S(2)}, u32[]{:S(2)}) collective-permute-start(f32[30,1024]{1,0:T(8,128)S(1)} %constant_dynamic-update-slice_fusion.h_ref), channel_id=1, source_target_pairs={{0,128},{64,192},{128,0},{192,64},{1,129},{65,193},{129,1},{193,65... | collective-permute-start | bytes 368648 | tf_op jit(solution)/shard_map/ppermute | solution.py:193
  65.4 0.7 copy-start.2
  73.8 0.7 copy-start.5
  74.4 0.7 copy-start.1
  82.7 0.6 copy-start.4
  83.4 0.7 copy-start
  99.9 16.2 %collective-permute-start.8 = (f32[30,512]{1,0:T(8,128)S(1)}, f32[30,512]{1,0:T(8,128)S(1)}, u32[]{:S(2)}, u32[]{:S(2)}) collective-permute-start(f32[30,512]{1,0:T(8,128)S(1)} %get-tuple-element.13), channel_id=1, source_target_pairs={{0,1},{1,2},{2,3},{3,4},{4,5},{5,6},{6,7},{7,8},{8,9},{9,10},{10,1... | collective-permute-start | bytes 184328 | tf_op jit(solution)/shard_map/ppermute | solution.py:200
  107.9 9.7 %collective-permute-start.9 = (f32[30,512]{1,0:T(8,128)S(1)}, f32[30,512]{1,0:T(8,128)S(1)}, u32[]{:S(2)}, u32[]{:S(2)}) collective-permute-start(f32[30,512]{1,0:T(8,128)S(1)} %get-tuple-element.14), channel_id=1, source_target_pairs={{1,0},{2,1},{3,2},{4,3},{5,4},{6,5},{7,6},{8,7},{9,8},{10,9},{11,1... | collective-permute-start | bytes 184328 | tf_op jit(solution)/shard_map/ppermute | solution.py:199

commit v2 on v1

v2 whole, which is shorter than its diff:
```python
import jax
import jax.numpy as jnp
from jax import lax
from jax.experimental import pallas as pl
from jax.experimental.pallas import tpu as pltpu
from jax.sharding import PartitionSpec as P


HALO = 512
MD = 30
SLOTS = 6
E = 1024
OWN = 3072
TERMS = 4
LANES = SLOTS * E
NN = (((1,), (0,)), ((), ()))
NT = (((1,), (1,)), ((), ()))
F32 = jnp.float32
BF16 = jnp.bfloat16
STEP = 512
VMEM = pl.BlockSpec(memory_space=pltpu.VMEM)
PARAMS = pltpu.CompilerParams(vmem_limit_bytes=16 << 20)


def split_hi_lo(x):
    hi = x.astype(BF16)
    lo = (x - hi.astype(F32)).astype(BF16)
    return hi, lo


def remap(links, odd):
    own = links - HALO
    mine = jnp.where(own < HALO, own, jnp.where(own < OWN - HALO, own + HALO, own - (OWN - 2 * HALO)))
    left = links + OWN + HALO * odd
    right = links - HALO * odd
    return jnp.where(links < HALO, left, jnp.where(links < HALO + OWN, mine, right))


def codes(faces):
    return faces >> 10, (faces >> 8) & 3, faces & 255


def one_hot(chunk_of, row, chunk):
    n = row.shape[1]
    ids = lax.broadcasted_iota(jnp.int32, (256, n), 0).astype(F32).astype(BF16)
    mine = jnp.where(chunk_of == chunk, row, -1).astype(F32).astype(BF16)
    return jnp.where(ids == mine, jnp.ones((), BF16), jnp.zeros((), BF16))


def fill(piece, t_ref, base, lane):
    n = piece.shape[0]
    hi, lo = split_hi_lo(piece)
    t_ref[base : base + n, lane : lane + 256] = hi
    t_ref[base + 32 : base + 32 + n, lane : lane + 256] = lo


def pick(got, quad):
    total = jnp.zeros((64, got.shape[1]), F32)
    for q in range(4):
        total = total + jnp.where(quad == q, got[q * 64 : (q + 1) * 64], 0.0)
    return total.astype(BF16)


def table_kernel(me_ref, modes_ref, terms_ref, values_ref, out_ref):
    me = me_ref[0]
    n = values_ref.shape[1]
    i_loc = modes_ref[0:1, :] - MD * me
    row = jnp.where((i_loc >= 0) & (i_loc < MD), terms_ref[...] * 32 + i_loc, -1)
    j = modes_ref[1:2, :]
    part = (j >= MD).astype(jnp.int32) + (j >= 2 * MD).astype(jnp.int32) + (j >= 3 * MD).astype(jnp.int32)
    col = (part ^ me) * 64 + (j - MD * part)
    rid = lax.broadcasted_iota(jnp.int32, (128, n), 0)
    cid = lax.broadcasted_iota(jnp.int32, (256, n), 0)
    cols = jnp.where((cid & ~32) == col, 1.0, 0.0).astype(BF16)
    left = jnp.where(rid == row, values_ref[...], 0.0)
    a = left.astype(BF16)
    rest = left - a.astype(F32)
    b = rest.astype(BF16)
    c = (rest - b.astype(F32)).astype(BF16)
    total = lax.dot_general(a, cols, NT, preferred_element_type=F32)
    total = total + lax.dot_general(b, cols, NT, preferred_element_type=F32)
    total = total + lax.dot_general(c, cols, NT, preferred_element_type=F32)
    hi, lo = split_hi_lo(total)
    out_ref[0:128, :] = hi
    out_ref[128:256, :] = lo


def coupling_table(me, pair_modes, pair_terms, pair_values):
    n = pair_values.shape[0]
    wide = -(-n // 128) * 128
    modes = jnp.pad(pair_modes, ((0, 0), (0, wide - n)))
    terms = jnp.pad(pair_terms, (0, wide - n)).reshape(1, wide)
    values = jnp.pad(pair_values, (0, wide - n)).reshape(1, wide)
    return pl.pallas_call(
        table_kernel,
        out_shape=jax.ShapeDtypeStruct((256, 256), BF16),
        in_specs=[pl.BlockSpec(memory_space=pltpu.SMEM)] + [VMEM] * 3,
        out_specs=VMEM,
        compiler_params=PARAMS,
    )(me, modes, terms, values)


def gather_body(piece, links_ref, out_ref, t_ref):
    for r in range(8):
        t_ref[r * 32 + 16 : r * 32 + 32, :] = jnp.zeros((16, 768), BF16)
    for c in range(3):
        for q in range(4):
            fill(piece(c, q), t_ref, q * 64, c * 256)
    for b in range(SLOTS):
        chunk_of, quad, row = codes(links_ref[b : b + 1, :])
        hot = jnp.concatenate([one_hot(chunk_of, row, c) for c in range(3)], axis=0)
        got = lax.dot_general(t_ref[...], hot, NN, preferred_element_type=F32)
        out_ref[:, b * E : (b + 1) * E] = pick(got, jnp.where(chunk_of < 3, quad, -1))


def gather_whole_kernel(x_ref, links_ref, out_ref, t_ref):
    def piece(c, q):
        first = HALO + (c - 1) * 1024 + q * 256 if c else q * 256 + (q // 2) * (OWN - 2 * HALO)
        return x_ref[:, first : first + 256]

    gather_body(piece, links_ref, out_ref, t_ref)


def gather_parts_kernel(rims_ref, inside_ref, links_ref, out_ref, t_ref):
    def piece(c, q):
        first = (c - 1) * 1024 + q * 256
        return inside_ref[:, first : first + 256] if c else rims_ref[:, q * 256 : (q + 1) * 256]

    gather_body(piece, links_ref, out_ref, t_ref)


def gather_own(links, *xs):
    return pl.pallas_call(
        gather_whole_kernel if len(xs) == 1 else gather_parts_kernel,
        out_shape=jax.ShapeDtypeStruct((64, LANES), BF16),
        in_specs=[VMEM] * (len(xs) + 1),
        out_specs=VMEM,
        scratch_shapes=[pltpu.VMEM((256, 768), BF16)],
        compiler_params=PARAMS,
    )(*xs, links)


def gather_halo_kernel(o0, o2, o13, inner, links_ref, out_ref, t_ref):
    for r in range(32):
        t_ref[r * 32 + 16 : r * 32 + 32, :] = jnp.zeros((16, 256), BF16)
    for d, (o, first) in enumerate(((o0, 0), (o13, 0), (o2, 0), (o13, MD))):
        for q in range(2):
            fill(o[first : first + MD, q * 256 : (q + 1) * 256], t_ref, (d * 4 + q) * 64, 0)
            fill(inner[d * MD : (d + 1) * MD, q * 256 : (q + 1) * 256], t_ref, (d * 4 + 2 + q) * 64, 0)
    for b in range(SLOTS):
        chunk_of, quad, row = codes(links_ref[b : b + 1, :])
        hot = one_hot(chunk_of, row, 3)
        for d in range(4):
            got = lax.dot_general(t_ref[d * 256 : (d + 1) * 256, :], hot, NN, preferred_element_type=F32)
            out_ref[d * 64 : (d + 1) * 64, b * E : (b + 1) * E] = pick(got, quad)


def gather_halo(o0, o2, o13, inner, links):
    return pl.pallas_call(
        gather_halo_kernel,
        out_shape=jax.ShapeDtypeStruct((256, LANES), BF16),
        in_specs=[VMEM] * 5,
        out_specs=VMEM,
        scratch_shapes=[pltpu.VMEM((1024, 256), BF16)],
        compiler_params=PARAMS,
    )(o0, o2, o13, inner, links)


def scatter_chunk(l_ref, links_ref, chunk):
    total = None
    for a in range(SLOTS):
        chunk_of, _, row = codes(links_ref[a : a + 1, :])
        hot = one_hot(chunk_of, row, chunk)
        part = lax.dot_general(l_ref[:, a * E : (a + 1) * E], hot, NT, preferred_element_type=F32)
        total = part if total is None else total + part
    return total


def element_kernel(g0, g1, g2, g3, gh, table_ref, mats_ref, links_ref, l_ref, rims_ref, y_ref):
    def one(i, carry):
        base = pl.multiple_of(i * STEP, STEP)
        for b in range(SLOTS):
            here = pl.ds(b * E + base, STEP)
            right = jnp.concatenate([g[:, here] for g in (g0, g1, g2, g3)], axis=0) + gh[:, here]
            got = lax.dot_general(table_ref[...], right, NN, preferred_element_type=F32)
            own = right[0:64].astype(F32)
            y_ref[b, 0:32] = own[0:32] + own[32:64]
            y_ref[b, 32:160] = got[0:128] + got[128:256]
        for a in range(SLOTS):
            acc = None
            for b in range(SLOTS):
                for k in range(TERMS + 1):
                    m = mats_ref[k, 6 * a + b : 6 * a + b + 1, pl.ds(base, STEP)]
                    term = m * y_ref[b, 32 * k : 32 * (k + 1)]
                    acc = term if acc is None else acc + term
            here = pl.ds(a * E + base, STEP)
            _, quad, _ = codes(links_ref[a : a + 1, pl.ds(base, STEP)])
            hi = acc.astype(BF16).astype(F32)
            lo = acc - hi
            for q in range(4):
                l_ref[q * 64 : q * 64 + 32, here] = jnp.where(quad == q, hi, 0.0).astype(BF16)
                l_ref[q * 64 + 32 : q * 64 + 64, here] = jnp.where(quad == q, lo, 0.0).astype(BF16)
        return carry

    lax.fori_loop(0, E // STEP, one, 0)
    total = scatter_chunk(l_ref, links_ref, 3)
    for q in range(4):
        both = total[q * 64 : q * 64 + 32] + total[q * 64 + 32 : q * 64 + 64]
        rims_ref[:, q * 256 : (q + 1) * 256] = both[0:MD]


def elements(gs, halo, table, mats, links):
    return pl.pallas_call(
        element_kernel,
        out_shape=(jax.ShapeDtypeStruct((256, LANES), BF16), jax.ShapeDtypeStruct((MD, 2 * HALO), F32)),
        in_specs=[VMEM] * 8,
        out_specs=(VMEM, VMEM),
        scratch_shapes=[pltpu.VMEM((SLOTS, 160, STEP), F32)],
        compiler_params=PARAMS,
    )(*gs, halo, table, mats, links)


def own_kernel(l_ref, links_ref, out_ref):
    for chunk in range(3):
        total = scatter_chunk(l_ref, links_ref, chunk)
        for q in range(4):
            both = total[q * 64 : q * 64 + 32] + total[q * 64 + 32 : q * 64 + 64]
            first = HALO + (chunk - 1) * 1024 + q * 256 if chunk else q * 256 + (q // 2) * (OWN - 2 * HALO)
            out_ref[:, first : first + 256] = both[0:MD]


def scatter_own(l, links):
    return pl.pallas_call(
        own_kernel,
        out_shape=jax.ShapeDtypeStruct((MD, OWN), F32),
        in_specs=[VMEM] * 2,
        out_specs=VMEM,
        compiler_params=PARAMS,
    )(l, links)


def finish_kernel(odd_ref, own_ref, out_in_ref, in_in_ref, out_ref):
    odd = odd_ref[0] == 1
    outer = out_in_ref[...]
    inner = in_in_ref[...]
    out_ref[:, HALO : OWN - HALO] = own_ref[:, HALO : OWN - HALO]
    out_ref[:, :HALO] = own_ref[:, :HALO] + jnp.where(odd, inner, outer)
    out_ref[:, OWN - HALO :] = own_ref[:, OWN - HALO :] + jnp.where(odd, outer, inner)


def finish(odd, own, outer, inner):
    return pl.pallas_call(
        finish_kernel,
        out_shape=jax.ShapeDtypeStruct((MD, OWN), F32),
        in_specs=[pl.BlockSpec(memory_space=pltpu.SMEM)] + [VMEM] * 3,
        out_specs=VMEM,
        compiler_params=PARAMS,
    )(odd, own, outer, inner)


def body(traces, elem_mats, face_links, pair_modes, pair_terms, pair_values):
    parts = lax.axis_size("space")
    me = lax.axis_index("mode").astype(jnp.int32).reshape(1)
    odd = lax.axis_index("space").astype(jnp.int32) % 2
    outer_pairs = [(i, i + 1) for i in range(1, parts - 1, 2)] + [(i + 1, i) for i in range(1, parts - 1, 2)]
    inner_pairs = [(i, i ^ 1) for i in range(parts)]
    near = [(i, i ^ 1) for i in range(4)]
    far = [(i, i ^ 2) for i in range(4)]
    links = remap(face_links, odd)
    rims = jnp.concatenate([traces[:, :HALO], traces[:, OWN - HALO :]], axis=1)
    x2a = lax.ppermute(rims, "mode", far)
    x1 = lax.ppermute(traces, "mode", near)
    o0 = lax.ppermute(lax.dynamic_slice_in_dim(rims, HALO * odd, HALO, axis=1), "space", outer_pairs)
    x2b = lax.ppermute(traces[:, HALO : OWN - HALO], "mode", far)
    x3a = lax.ppermute(x2a, "mode", near)
    o2 = lax.ppermute(o0, "mode", far)
    x3b = lax.ppermute(x2b, "mode", near)
    o13 = lax.ppermute(jnp.concatenate([o0, o2], axis=0), "mode", near)
    near_rims = jnp.concatenate([x1[:, :HALO], x1[:, OWN - HALO :]], axis=1)
    all_rims = jnp.concatenate([rims, near_rims, x2a, x3a], axis=0)
    inner = lax.ppermute(lax.dynamic_slice_in_dim(all_rims, HALO * (1 - odd), HALO, axis=1), "space", inner_pairs)
    table = coupling_table(me, pair_modes, pair_terms, pair_values)
    g0 = gather_own(links, traces)
    g1 = gather_own(links, x1)
    g2 = gather_own(links, x2a, x2b)
    g3 = gather_own(links, x3a, x3b)
    halo = gather_halo(o0, o2, o13, inner, links)
    local, back = elements((g0, g1, g2, g3), halo, table, elem_mats, links)
    back_outer = lax.ppermute(back[:, :HALO], "space", outer_pairs)
    back_inner = lax.ppermute(back[:, HALO:], "space", inner_pairs)
    own = scatter_own(local, links)
    return finish(odd.reshape(1), own, back_outer, back_inner)


def solution(mesh):
    return jax.shard_map(
        body,
        mesh=mesh,
        in_specs=(P("mode", "space"), P(None, None, "space"), P(None, "space"), P(), P(), P()),
        out_specs=P("mode", "space"),
        check_vma=False,
    )
```

time: 121 us -> 75.3 us (0.62)
  the two profiles are of different devices: /device:TPU:7 before, /device:TPU:6 now
where the time goes in v2:
time: 75.3 us; the launch traced here: 74.9 us
  starting transfers between devices  25 us (33%)
  Pallas kernels  23.2 us (31%)
  waiting for transfers between devices  20.3 us (27%)
  local copies, waits for them, and re-layouts  5.04 us (7%)
  other arithmetic  0.98 us (1%)
    ppermute x1, waiting for transfers between devices, body(): lax.ppermute(lax.dynamic_slice_in_dim(rims, HALO * odd, HALO, axis=1), 's...  11.5 us
    pallas_call x4, Pallas kernels, gather_own(): pl.pallas_call(gather_whole_kernel if len(xs) == 1 else gather_parts_kern...  10.7 us
    ppermute x1, starting transfers between devices, body(): lax.ppermute(lax.dynamic_slice_in_dim(rims, HALO * odd, HALO, axis=1), 's...  9.13 us
    ppermute x1, starting transfers between devices, body(): back_outer = lax.ppermute(back[:, :HALO], 'space', outer_pairs)  5.99 us
    ppermute x1, waiting for transfers between devices, body(): x3a = lax.ppermute(x2a, 'mode', near)  4.94 us
    pallas_call x1, Pallas kernels, elements(): pl.pallas_call(element_kernel, out_shape=(jax.ShapeDtypeStruct((256, LANE...  4.38 us
    ppermute x1, waiting for transfers between devices, body(): back_outer = lax.ppermute(back[:, :HALO], 'space', outer_pairs)  3.84 us
    pallas_call x1, Pallas kernels, gather_halo(): pl.pallas_call(gather_halo_kernel, out_shape=jax.ShapeDtypeStruct((256, L...  3.76 us
  transfers between devices with their start and end apart: 11, of which 3 were waited for; matrix products, arithmetic and copies ran while one was open for 7% of the time, Pallas kernels for 19%

profile of v2, /device:TPU:6, one launch (start us, length us, event | category | flops | bytes accessed | tf_op | source)
XLA Modules:
  0.0 74.9 jit_solution(2921106807940146721)
XLA Ops:
  0.0 1.9 %collective-permute-start = (f32[30,3072]{1,0:T(8,128)}, f32[30,3072]{1,0:T(8,128)S(1)}, u32[]{:S(2)}, u32[]{:S(2)}) collective-permute-start(f32[30,3072]{1,0:T(8,128)} %x_ref.1), channel_id=1, source_target_pairs={{0,64},{64,0},{128,192},{192,128},{1,65},{65,1},{129,193},{193,129... | collective-permute-start | bytes 1105928 | tf_op jit(solution)/shard_map/ppermute | solution.py:272
  1.9 1.0 %slice.23 = f32[30,2048]{1,0:T(8,128)S(1)} slice(f32[30,3072]{1,0:T(8,128)} %x_ref.1), slice={[0:30], [512:2560]} | slice | bytes 491520 | tf_op jit(solution)/shard_map/slice | solution.py:274
  2.9 3.4 %collective-permute-start.2 = (f32[30,2048]{1,0:T(8,128)S(1)}, f32[30,2048]{1,0:T(8,128)S(1)}, u32[]{:S(2)}, u32[]{:S(2)}) collective-permute-start(f32[30,2048]{1,0:T(8,128)S(1)} %slice.23), channel_id=1, source_target_pairs={{0,128},{64,192},{128,0},{192,64},{1,129},{65,193},{129,1},{193,65... | collective-permute-start | bytes 737288 | tf_op jit(solution)/shard_map/ppermute | solution.py:274
  6.3 0.9 %fusion.9 = (f32[30,512]{1,0:T(8,128)S(1)}, f32[30,512]{1,0:T(8,128)S(1)}) fusion(f32[30,3072]{1,0:T(8,128)} %x_ref.1), kind=kLoop, calls=%fused_computation.21 | loop fusion | bytes 245760 | tf_op jit(solution)/shard_map/slice | solution.py:270
  7.3 9.1 %collective-permute-start.5 = (f32[30,512]{1,0:T(8,128)S(1)}, f32[30,512]{1,0:T(8,128)S(1)}, u32[]{:S(2)}, u32[]{:S(2)}) collective-permute-start(f32[30,512]{1,0:T(8,128)S(1)} %fusion.5), channel_id=1, source_target_pairs={{1,2},{3,4},{5,6},{7,8},{9,10},{11,12},{13,14},{15,16},{17,18},{19... | collective-permute-start | bytes 184328 | tf_op jit(solution)/shard_map/ppermute | solution.py:273
  16.5 0.7 pad.13
  17.9 0.7 pad.12.modes_ref
  18.6 11.5 %collective-permute-done.5.o0 = f32[30,512]{1,0:T(8,128)S(1)} collective-permute-done((f32[30,512]{1,0:T(8,128)S(1)}, f32[30,512]{1,0:T(8,128)S(1)}, u32[]{:S(2)}, u32[]{:S(2)}) %collective-permute-start.5) | collective-permute-done | bytes 61472 | tf_op jit(solution)/shard_map/ppermute | solution.py:273
  30.2 2.5 %collective-permute-start.3 = (f32[30,1024]{1,0:T(8,128)S(1)}, f32[30,1024]{1,0:T(8,128)S(1)}, u32[]{:S(2)}, u32[]{:S(2)}) collective-permute-start(f32[30,1024]{1,0:T(8,128)S(1)} %collective-permute-done.1.rims_ref), channel_id=1, source_target_pairs={{0,64},{64,0},{128,192},{192,128},{1,65},{65,1},{129,193},{193,129... | collective-permute-start | bytes 368648 | tf_op jit(solution)/shard_map/ppermute | solution.py:275
  32.8 4.9 %collective-permute-done.3.rims_ref = f32[30,1024]{1,0:T(8,128)S(1)} collective-permute-done((f32[30,1024]{1,0:T(8,128)S(1)}, f32[30,1024]{1,0:T(8,128)S(1)}, u32[]{:S(2)}, u32[]{:S(2)}) %collective-permute-start.3) | collective-permute-done | bytes 122912 | tf_op jit(solution)/shard_map/ppermute | solution.py:275
  38.0 1.6 %collective-permute-start.7 = (f32[60,512]{1,0:T(8,128)S(1)}, f32[60,512]{1,0:T(8,128)S(1)}, u32[]{:S(2)}, u32[]{:S(2)}) collective-permute-start(f32[60,512]{1,0:T(8,128)S(1)} %pad_maximum_fusion.1), channel_id=1, source_target_pairs={{0,64},{64,0},{128,192},{192,128},{1,65},{65,1},{129,193},{193,129... | collective-permute-start | bytes 368648 | tf_op jit(solution)/shard_map/ppermute | solution.py:278
  39.6 0.8 %fusion.7.links_ref = s32[6,1024]{1,0:T(8,128)S(1)} fusion(s32[6,1024]{1,0:T(8,128)} %param.8, s32[]{:T(128)S(6)} %mul.8), kind=kLoop, calls=%fused_computation.19 | loop fusion | flops 79872 | bytes 49156 | tf_op jit(solution)/shard_map/jit(_where)/select_n | solution.py:36
  40.4 1.0 %copy-done = f32[30,3072]{1,0:T(8,128)S(1)} copy-done((f32[30,3072]{1,0:T(8,128)S(1)}, f32[30,3072]{1,0:T(8,128)}, u32[]{:S(2)}) %copy-start) | copy-done | bytes 368664
  41.4 2.7 %shard_map.64.g0 = bf16[64,6144]{1,0:T(8,128)(2,1)S(1)} custom-call(f32[30,3072]{1,0:T(8,128)S(1)} %copy-done, s32[6,1024]{1,0:T(8,128)S(1)} %fusion.7.links_ref), custom_call_target="tpu_custom_call" | custom-call | tf_op jit(solution)/shard_map/pallas_call | solution.py:133
  44.0 1.0 %shard_map.69.table_ref = bf16[256,256]{1,0:T(8,128)(2,1)S(1)} custom-call(s32[1]{0:T(128)} %bitcast.1.me_ref, s32[2,1536]{1,0:T(2,128)S(1)} %pad.12.modes_ref, s32[1,1536]{1,0:T(1,128)S(1)} %reshape.14.terms_ref, f32[1,1536]{1,0:T(1,128)S(1)} %reshape.15.values_ref), custom_call_target="tpu_custom_call" | custom-call | tf_op jit(solution)/shard_map/pallas_call | solution.py:94
  45.0 2.7 %shard_map.66.g2 = bf16[64,6144]{1,0:T(8,128)(2,1)S(1)} custom-call(f32[30,1024]{1,0:T(8,128)S(1)} %collective-permute-done.1.rims_ref, f32[30,2048]{1,0:T(8,128)S(1)} %collective-permute-done.2.inside_ref, s32[6,1024]{1,0:T(8,128)S(1)} %fusion.7.links_ref), custom_call_target="tpu_custom_call" | custom-call | tf_op jit(solution)/shard_map/pallas_call | solution.py:133
  47.7 2.7 %shard_map.65.g1 = bf16[64,6144]{1,0:T(8,128)(2,1)S(1)} custom-call(f32[30,3072]{1,0:T(8,128)S(1)} %collective-permute-done.x_ref, s32[6,1024]{1,0:T(8,128)S(1)} %fusion.7.links_ref), custom_call_target="tpu_custom_call" | custom-call | tf_op jit(solution)/shard_map/pallas_call | solution.py:133
  50.4 2.7 %shard_map.67.g3 = bf16[64,6144]{1,0:T(8,128)(2,1)S(1)} custom-call(f32[30,1024]{1,0:T(8,128)S(1)} %collective-permute-done.3.rims_ref, f32[30,2048]{1,0:T(8,128)S(1)} %collective-permute-done.4.inside_ref, s32[6,1024]{1,0:T(8,128)S(1)} %fusion.7.links_ref), custom_call_target="tpu_custom_call" | custom-call | tf_op jit(solution)/shard_map/pallas_call | solution.py:133
  53.1 3.8 %shard_map.68.gh = bf16[256,6144]{1,0:T(8,128)(2,1)S(1)} custom-call(f32[30,512]{1,0:T(8,128)S(1)} %collective-permute-done.5.o0, f32[30,512]{1,0:T(8,128)S(1)} %collective-permute-done.6.o2, f32[60,512]{1,0:T(8,128)S(1)} %collective-permute-done.7.o13, f32[120,512]{1,0:T(8,128)S(1)} %collective-permute-done.8.inner, s32[6,1024]{1,0:T(8,128)S(1)} %fusion.7.links_ref), custom_call_target="tpu_custom_call" | custom-call | tf_op jit(solution)/shard_map/pallas_call | solution.py:159
  56.9 4.4 %shard_map.70 = (bf16[256,6144]{1,0:T(8,128)(2,1)S(1)}, f32[30,1024]{1,0:T(8,128)S(1)}) custom-call(bf16[64,6144]{1,0:T(8,128)(2,1)S(1)} %shard_map.64.g0, bf16[64,6144]{1,0:T(8,128)(2,1)S(1)} %shard_map.65.g1, bf16[64,6144]{1,0:T(8,128)(2,1)S(1)} %shard_map.66.g2, bf16[64,6144]{1,0:T(8,128)(2,1)S(1)} %shard_map.67.g3, bf16[256,6144]{1,0:T(8,128)(2,1)S(1)} %shard_map.68.gh, ...), custom_call_target="tpu_custom_call" | custom-call | tf_op jit(solution)/shard_map/pallas_call | solution.py:213
  61.6 6.0 %collective-permute-start.9 = (f32[30,512]{1,0:T(8,128)S(1)}, f32[30,512]{1,0:T(8,128)S(1)}, u32[]{:S(2)}, u32[]{:S(2)}) collective-permute-start(f32[30,512]{1,0:T(8,128)S(1)} %get-tuple-element.14), channel_id=1, source_target_pairs={{1,2},{3,4},{5,6},{7,8},{9,10},{11,12},{13,14},{15,16},{17,18},{19... | collective-permute-start | bytes 184328 | tf_op jit(solution)/shard_map/ppermute | solution.py:289
  67.6 2.6 %shard_map.71.own_ref = f32[30,3072]{1,0:T(8,128)S(1)} custom-call(bf16[256,6144]{1,0:T(8,128)(2,1)S(1)} %get-tuple-element.7.l_ref, s32[6,1024]{1,0:T(8,128)S(1)} %fusion.7.links_ref), custom_call_target="tpu_custom_call" | custom-call | tf_op jit(solution)/shard_map/pallas_call | solution.py:233
  70.2 3.8 %collective-permute-done.9.out_in_ref = f32[30,512]{1,0:T(8,128)S(1)} collective-permute-done((f32[30,512]{1,0:T(8,128)S(1)}, f32[30,512]{1,0:T(8,128)S(1)}, u32[]{:S(2)}, u32[]{:S(2)}) %collective-permute-start.9) | collective-permute-done | bytes 61472 | tf_op jit(solution)/shard_map/ppermute | solution.py:289
  74.1 0.8 %shard_map.72 = f32[30,3072]{1,0:T(8,128)} custom-call(s32[1]{0:T(128)} %bitcast.odd_ref, f32[30,3072]{1,0:T(8,128)S(1)} %shard_map.71.own_ref, f32[30,512]{1,0:T(8,128)S(1)} %collective-permute-done.9.out_in_ref, f32[30,512]{1,0:T(8,128)S(1)} %collective-permute-done.10.in_in_ref), custom_call_target="tpu_custom_call" | custom-call | tf_op jit(solution)/shard_map/pallas_call | solution.py:252
  (25 shorter events, 1.6 us)
Async XLA Ops:
  0.0 32.7 %collective-permute-start = (f32[30,3072]{1,0:T(8,128)}, f32[30,3072]{1,0:T(8,128)S(1)}, u32[]{:S(2)}, u32[]{:S(2)}) collective-permute-start(f32[30,3072]{1,0:T(8,128)} %x_ref.1), channel_id=1, source_target_pairs={{0,64},{64,0},{128,192},{192,128},{1,65},{65,1},{129,193},{193,129... | collective-permute-start | bytes 1105928 | tf_op jit(solution)/shard_map/ppermute | solution.py:272
  2.9 29.7 %collective-permute-start.2 = (f32[30,2048]{1,0:T(8,128)S(1)}, f32[30,2048]{1,0:T(8,128)S(1)}, u32[]{:S(2)}, u32[]{:S(2)}) collective-permute-start(f32[30,2048]{1,0:T(8,128)S(1)} %slice.23), channel_id=1, source_target_pairs={{0,128},{64,192},{128,0},{192,64},{1,129},{65,193},{129,1},{193,65... | collective-permute-start | bytes 737288 | tf_op jit(solution)/shard_map/ppermute | solution.py:274
  7.2 23.0 %collective-permute-start.1 = (f32[30,1024]{1,0:T(8,128)S(1)}, f32[30,1024]{1,0:T(8,128)S(1)}, u32[]{:S(2)}, u32[]{:S(2)}) collective-permute-start(f32[30,1024]{1,0:T(8,128)S(1)} %pad_maximum_fusion), channel_id=1, source_target_pairs={{0,128},{64,192},{128,0},{192,64},{1,129},{65,193},{129,1},{193,65... | collective-permute-start | bytes 368648 | tf_op jit(solution)/shard_map/ppermute | solution.py:271
  7.3 22.8 %collective-permute-start.5 = (f32[30,512]{1,0:T(8,128)S(1)}, f32[30,512]{1,0:T(8,128)S(1)}, u32[]{:S(2)}, u32[]{:S(2)}) collective-permute-start(f32[30,512]{1,0:T(8,128)S(1)} %fusion.5), channel_id=1, source_target_pairs={{1,2},{3,4},{5,6},{7,8},{9,10},{11,12},{13,14},{15,16},{17,18},{19... | collective-permute-start | bytes 184328 | tf_op jit(solution)/shard_map/ppermute | solution.py:273
  30.2 7.8 %collective-permute-start.6 = (f32[30,512]{1,0:T(8,128)S(1)}, f32[30,512]{1,0:T(8,128)S(1)}, u32[]{:S(2)}, u32[]{:S(2)}) collective-permute-start(f32[30,512]{1,0:T(8,128)S(1)} %collective-permute-done.5.o0), channel_id=1, source_target_pairs={{0,128},{64,192},{128,0},{192,64},{1,129},{65,193},{129,1},{193,65... | collective-permute-start | bytes 184328 | tf_op jit(solution)/shard_map/ppermute | solution.py:276
  30.2 7.5 %collective-permute-start.3 = (f32[30,1024]{1,0:T(8,128)S(1)}, f32[30,1024]{1,0:T(8,128)S(1)}, u32[]{:S(2)}, u32[]{:S(2)}) collective-permute-start(f32[30,1024]{1,0:T(8,128)S(1)} %collective-permute-done.1.rims_ref), channel_id=1, source_target_pairs={{0,64},{64,0},{128,192},{192,128},{1,65},{65,1},{129,193},{193,129... | collective-permute-start | bytes 368648 | tf_op jit(solution)/shard_map/ppermute | solution.py:275
  32.7 17.7 %collective-permute-start.4 = (f32[30,2048]{1,0:T(8,128)S(1)}, f32[30,2048]{1,0:T(8,128)S(1)}, u32[]{:S(2)}, u32[]{:S(2)}) collective-permute-start(f32[30,2048]{1,0:T(8,128)S(1)} %collective-permute-done.2.inside_ref), channel_id=1, source_target_pairs={{0,64},{64,0},{128,192},{192,128},{1,65},{65,1},{129,193},{193,129... | collective-permute-start | bytes 737288 | tf_op jit(solution)/shard_map/ppermute | solution.py:277
  37.9 15.2 %collective-permute-start.8 = (f32[120,512]{1,0:T(8,128)S(1)}, f32[120,512]{1,0:T(8,128)S(1)}, u32[]{:S(2)}, u32[]{:S(2)}) collective-permute-start(f32[120,512]{1,0:T(8,128)S(1)} %fusion.3), channel_id=1, source_target_pairs={{0,1},{1,0},{2,3},{3,2},{4,5},{5,4},{6,7},{7,6},{8,9},{9,8},{10,11... | collective-permute-start | bytes 737288 | tf_op jit(solution)/shard_map/ppermute | solution.py:281
  38.0 15.1 %collective-permute-start.7 = (f32[60,512]{1,0:T(8,128)S(1)}, f32[60,512]{1,0:T(8,128)S(1)}, u32[]{:S(2)}, u32[]{:S(2)}) collective-permute-start(f32[60,512]{1,0:T(8,128)S(1)} %pad_maximum_fusion.1), channel_id=1, source_target_pairs={{0,64},{64,0},{128,192},{192,128},{1,65},{65,1},{129,193},{193,129... | collective-permute-start | bytes 368648 | tf_op jit(solution)/shard_map/ppermute | solution.py:278
  40.4 1.0 %copy-start = (f32[30,3072]{1,0:T(8,128)S(1)}, f32[30,3072]{1,0:T(8,128)}, u32[]{:S(2)}) copy-start(f32[30,3072]{1,0:T(8,128)} %x_ref.1) | copy-start | bytes 1105924
  47.7 9.2 %copy-start.1 = (f32[5,36,1024]{2,1,0:T(8,128)S(1)}, f32[5,36,1024]{2,1,0:T(8,128)}, u32[]{:S(2)}) copy-start(f32[5,36,1024]{2,1,0:T(8,128)} %mats_ref.1) | copy-start | bytes 2211844
  61.3 8.9 %collective-permute-start.10 = (f32[30,512]{1,0:T(8,128)S(1)}, f32[30,512]{1,0:T(8,128)S(1)}, u32[]{:S(2)}, u32[]{:S(2)}) collective-permute-start(f32[30,512]{1,0:T(8,128)S(1)} %get-tuple-element.13), channel_id=1, source_target_pairs={{0,1},{1,0},{2,3},{3,2},{4,5},{5,4},{6,7},{7,6},{8,9},{9,8},{10,11... | collective-permute-start | bytes 184328 | tf_op jit(solution)/shard_map/ppermute | solution.py:290
  61.6 12.5 %collective-permute-start.9 = (f32[30,512]{1,0:T(8,128)S(1)}, f32[30,512]{1,0:T(8,128)S(1)}, u32[]{:S(2)}, u32[]{:S(2)}) collective-permute-start(f32[30,512]{1,0:T(8,128)S(1)} %get-tuple-element.14), channel_id=1, source_target_pairs={{1,2},{3,4},{5,6},{7,8},{9,10},{11,12},{13,14},{15,16},{17,18},{19... | collective-permute-start | bytes 184328 | tf_op jit(solution)/shard_map/ppermute | solution.py:289

commit v3 on v2

v3 whole, which is shorter than its diff:
```python
import functools

import jax
import jax.numpy as jnp
from jax import lax
from jax.experimental import pallas as pl
from jax.experimental.pallas import tpu as pltpu
from jax.sharding import PartitionSpec as P


HALO = 512
MD = 30
SLOTS = 6
E = 1024
OWN = 3072
TERMS = 4
LANES = SLOTS * E
NN = (((1,), (0,)), ((), ()))
NT = (((1,), (1,)), ((), ()))
F32 = jnp.float32
BF16 = jnp.bfloat16
STEP = 512
VMEM = pl.BlockSpec(memory_space=pltpu.VMEM)
PARAMS = pltpu.CompilerParams(vmem_limit_bytes=16 << 20)


def split_hi_lo(x):
    hi = x.astype(BF16)
    lo = (x - hi.astype(F32)).astype(BF16)
    return hi, lo


def codes(links, odd):
    own = links - HALO
    mine = jnp.where(own < HALO, own, jnp.where(own < OWN - HALO, own + HALO, own - (OWN - 2 * HALO)))
    left = links + OWN + HALO * odd
    right = links - HALO * odd
    faces = jnp.where(links < HALO, left, jnp.where(links < HALO + OWN, mine, right))
    return faces >> 10, (faces >> 8) & 3, faces & 255


def one_hot(chunk_of, row, chunk):
    n = row.shape[1]
    ids = lax.broadcasted_iota(jnp.int32, (256, n), 0).astype(F32).astype(BF16)
    mine = jnp.where(chunk_of == chunk, row, -1).astype(F32).astype(BF16)
    return jnp.where(ids == mine, jnp.ones((), BF16), jnp.zeros((), BF16))


def fill(piece, t_ref, base, lane):
    n = piece.shape[0]
    hi, lo = split_hi_lo(piece)
    t_ref[base : base + n, lane : lane + 256] = hi
    t_ref[base + 32 : base + 32 + n, lane : lane + 256] = lo


def pick(got, quad):
    total = jnp.zeros((64, got.shape[1]), F32)
    for q in range(4):
        total = total + jnp.where(quad == q, got[q * 64 : (q + 1) * 64], 0.0)
    return total.astype(BF16)


def table_kernel(me_ref, modes_ref, terms_ref, values_ref, out_ref, ids_ref, v_ref):
    me = me_ref[0]
    n = values_ref.shape[1]
    wide = v_ref.shape[1]
    ids_ref[...] = jnp.full(ids_ref.shape, -1, jnp.int32)
    v_ref[...] = jnp.zeros(v_ref.shape, F32)
    v_ref[0:1, 0:n] = values_ref[...]
    i_loc = modes_ref[0:1, :] - MD * me
    ids_ref[0:1, 0:n] = jnp.where((i_loc >= 0) & (i_loc < MD), terms_ref[...] * 32 + i_loc, -1)
    j = modes_ref[1:2, :]
    part = (j >= MD).astype(jnp.int32) + (j >= 2 * MD).astype(jnp.int32) + (j >= 3 * MD).astype(jnp.int32)
    ids_ref[1:2, 0:n] = (part ^ me) * 64 + (j - MD * part)
    rid = lax.broadcasted_iota(jnp.int32, (128, wide), 0)
    cid = lax.broadcasted_iota(jnp.int32, (256, wide), 0)
    cols = jnp.where((cid & ~32) == ids_ref[1:2, :], 1.0, 0.0).astype(BF16)
    left = jnp.where(rid == ids_ref[0:1, :], v_ref[0:1, :], 0.0)
    a = left.astype(BF16)
    rest = left - a.astype(F32)
    b = rest.astype(BF16)
    c = (rest - b.astype(F32)).astype(BF16)
    total = lax.dot_general(a, cols, NT, preferred_element_type=F32)
    total = total + lax.dot_general(b, cols, NT, preferred_element_type=F32)
    total = total + lax.dot_general(c, cols, NT, preferred_element_type=F32)
    hi, lo = split_hi_lo(total)
    out_ref[0:128, :] = hi
    out_ref[128:256, :] = lo


SMEM = pl.BlockSpec(memory_space=pltpu.SMEM)


def coupling_table(me, pair_modes, pair_terms, pair_values):
    n = pair_values.shape[0]
    wide = -(-n // 128) * 128
    return pl.pallas_call(
        table_kernel,
        out_shape=jax.ShapeDtypeStruct((256, 256), BF16),
        in_specs=[SMEM] + [VMEM] * 3,
        out_specs=VMEM,
        scratch_shapes=[pltpu.VMEM((8, wide), jnp.int32), pltpu.VMEM((8, wide), F32)],
        compiler_params=PARAMS,
    )(me, pair_modes, pair_terms.reshape(1, n), pair_values.reshape(1, n))


def gather_body(piece, odd_ref, links_ref, out_ref, t_ref):
    for r in range(8):
        t_ref[r * 32 + 16 : r * 32 + 32, :] = jnp.zeros((16, 768), BF16)
    for c in range(3):
        for q in range(4):
            fill(piece(c, q), t_ref, q * 64, c * 256)
    for b in range(SLOTS):
        chunk_of, quad, row = codes(links_ref[b : b + 1, :], odd_ref[0])
        hot = jnp.concatenate([one_hot(chunk_of, row, c) for c in range(3)], axis=0)
        got = lax.dot_general(t_ref[...], hot, NN, preferred_element_type=F32)
        out_ref[:, b * E : (b + 1) * E] = pick(got, jnp.where(chunk_of < 3, quad, -1))


def gather_whole_kernel(odd_ref, x_ref, links_ref, out_ref, t_ref):
    def piece(c, q):
        first = HALO + (c - 1) * 1024 + q * 256 if c else q * 256 + (q // 2) * (OWN - 2 * HALO)
        return x_ref[:, first : first + 256]

    gather_body(piece, odd_ref, links_ref, out_ref, t_ref)


def gather_parts_kernel(odd_ref, rims_ref, inside_ref, links_ref, out_ref, t_ref):
    def piece(c, q):
        first = (c - 1) * 1024 + q * 256
        return inside_ref[:, first : first + 256] if c else rims_ref[:, q * 256 : (q + 1) * 256]

    gather_body(piece, odd_ref, links_ref, out_ref, t_ref)


def gather_own(odd, links, *xs):
    return pl.pallas_call(
        gather_whole_kernel if len(xs) == 1 else gather_parts_kernel,
        out_shape=jax.ShapeDtypeStruct((64, LANES), BF16),
        in_specs=[SMEM] + [VMEM] * (len(xs) + 1),
        out_specs=VMEM,
        scratch_shapes=[pltpu.VMEM((256, 768), BF16)],
        compiler_params=PARAMS,
    )(odd, *xs, links)


def gather_halo_kernel(half, odd_ref, outer_ref, inner_ref, links_ref, out_ref, t_ref):
    for r in range(16):
        t_ref[r * 32 + 16 : r * 32 + 32, :] = jnp.zeros((16, 256), BF16)
    for d in range(2):
        for q in range(2):
            here = slice(q * 256, (q + 1) * 256)
            fill(outer_ref[d * MD : (d + 1) * MD, here], t_ref, (d * 4 + q) * 64, 0)
            first = (2 * half + d) * MD
            fill(inner_ref[first : first + MD, here], t_ref, (d * 4 + 2 + q) * 64, 0)
    for b in range(SLOTS):
        chunk_of, quad, row = codes(links_ref[b : b + 1, :], odd_ref[0])
        hot = one_hot(chunk_of, row, 3)
        for d in range(2):
            got = lax.dot_general(t_ref[d * 256 : (d + 1) * 256, :], hot, NN, preferred_element_type=F32)
            out_ref[d * 64 : (d + 1) * 64, b * E : (b + 1) * E] = pick(got, quad)


def gather_halo(odd, links, outer, inner, half):
    return pl.pallas_call(
        functools.partial(gather_halo_kernel, half),
        out_shape=jax.ShapeDtypeStruct((128, LANES), BF16),
        in_specs=[SMEM] + [VMEM] * 3,
        out_specs=VMEM,
        scratch_shapes=[pltpu.VMEM((512, 256), BF16)],
        compiler_params=PARAMS,
    )(odd, outer, inner, links)


def scatter_chunk(odd_ref, l_ref, links_ref, chunk):
    total = None
    for a in range(SLOTS):
        chunk_of, _, row = codes(links_ref[a : a + 1, :], odd_ref[0])
        hot = one_hot(chunk_of, row, chunk)
        part = lax.dot_general(l_ref[:, a * E : (a + 1) * E], hot, NT, preferred_element_type=F32)
        total = part if total is None else total + part
    return total


def element_kernel(odd_ref, g0, g1, g2, g3, ha, hb, table_ref, mats_ref, links_ref, l_ref, outer_ref, inner_ref, y_ref):
    def one(i, carry):
        base = pl.multiple_of(i * STEP, STEP)
        for b in range(SLOTS):
            here = pl.ds(b * E + base, STEP)
            right = jnp.concatenate(
                [
                    g0[:, here] + ha[0:64, here],
                    g1[:, here] + hb[0:64, here],
                    g2[:, here] + ha[64:128, here],
                    g3[:, here] + hb[64:128, here],
                ],
                axis=0,
            )
            got = lax.dot_general(table_ref[...], right, NN, preferred_element_type=F32)
            own = right[0:64].astype(F32)
            y_ref[b, 0:32] = own[0:32] + own[32:64]
            y_ref[b, 32:160] = got[0:128] + got[128:256]
        for a in range(SLOTS):
            acc = None
            for b in range(SLOTS):
                for k in range(TERMS + 1):
                    m = mats_ref[k, 6 * a + b : 6 * a + b + 1, pl.ds(base, STEP)]
                    term = m * y_ref[b, 32 * k : 32 * (k + 1)]
                    acc = term if acc is None else acc + term
            here = pl.ds(a * E + base, STEP)
            _, quad, _ = codes(links_ref[a : a + 1, pl.ds(base, STEP)], odd_ref[0])
            hi = acc.astype(BF16).astype(F32)
            lo = acc - hi
            for q in range(4):
                l_ref[q * 64 : q * 64 + 32, here] = jnp.where(quad == q, hi, 0.0).astype(BF16)
                l_ref[q * 64 + 32 : q * 64 + 64, here] = jnp.where(quad == q, lo, 0.0).astype(BF16)
        return carry

    lax.fori_loop(0, E // STEP, one, 0)
    total = scatter_chunk(odd_ref, l_ref, links_ref, 3)
    for q in range(4):
        both = total[q * 64 : q * 64 + 32] + total[q * 64 + 32 : q * 64 + 64]
        ref = inner_ref if q // 2 else outer_ref
        ref[:, (q % 2) * 256 : (q % 2 + 1) * 256] = both[0:MD]


def elements(odd, gs, halos, table, mats, links):
    rim = jax.ShapeDtypeStruct((MD, HALO), F32)
    return pl.pallas_call(
        element_kernel,
        out_shape=(jax.ShapeDtypeStruct((256, LANES), BF16), rim, rim),
        in_specs=[SMEM] + [VMEM] * 9,
        out_specs=(VMEM, VMEM, VMEM),
        scratch_shapes=[pltpu.VMEM((SLOTS, 160, STEP), F32)],
        compiler_params=PARAMS,
    )(odd, *gs, *halos, table, mats, links)


def own_kernel(odd_ref, l_ref, links_ref, out_ref):
    for chunk in range(3):
        total = scatter_chunk(odd_ref, l_ref, links_ref, chunk)
        for q in range(4):
            both = total[q * 64 : q * 64 + 32] + total[q * 64 + 32 : q * 64 + 64]
            first = HALO + (chunk - 1) * 1024 + q * 256 if chunk else q * 256 + (q // 2) * (OWN - 2 * HALO)
            out_ref[:, first : first + 256] = both[0:MD]


def scatter_own(odd, l, links):
    return pl.pallas_call(
        own_kernel,
        out_shape=jax.ShapeDtypeStruct((MD, OWN), F32),
        in_specs=[SMEM] + [VMEM] * 2,
        out_specs=VMEM,
        compiler_params=PARAMS,
    )(odd, l, links)


def finish_kernel(odd_ref, own_ref, out_in_ref, in_in_ref, out_ref):
    odd = odd_ref[0] == 1
    outer = out_in_ref[...]
    inner = in_in_ref[...]
    out_ref[:, HALO : OWN - HALO] = own_ref[:, HALO : OWN - HALO]
    out_ref[:, :HALO] = own_ref[:, :HALO] + jnp.where(odd, inner, outer)
    out_ref[:, OWN - HALO :] = own_ref[:, OWN - HALO :] + jnp.where(odd, outer, inner)


def finish(odd, own, outer, inner):
    return pl.pallas_call(
        finish_kernel,
        out_shape=jax.ShapeDtypeStruct((MD, OWN), F32),
        in_specs=[pl.BlockSpec(memory_space=pltpu.SMEM)] + [VMEM] * 3,
        out_specs=VMEM,
        compiler_params=PARAMS,
    )(odd, own, outer, inner)


def body(traces, elem_mats, face_links, pair_modes, pair_terms, pair_values):
    parts = lax.axis_size("space")
    me = lax.axis_index("mode").astype(jnp.int32).reshape(1)
    odd = lax.axis_index("space").astype(jnp.int32) % 2
    outer_pairs = [(i, i + 1) for i in range(1, parts - 1, 2)] + [(i + 1, i) for i in range(1, parts - 1, 2)]
    inner_pairs = [(i, i ^ 1) for i in range(parts)]
    near = [(i, i ^ 1) for i in range(4)]
    far = [(i, i ^ 2) for i in range(4)]
    links = face_links
    side = odd.reshape(1)
    rims = jnp.concatenate([traces[:, :HALO], traces[:, OWN - HALO :]], axis=1)
    inside = traces[:, HALO : OWN - HALO]
    x2a = lax.ppermute(rims, "mode", far)
    x1 = lax.ppermute(traces, "mode", near)
    x2b = lax.ppermute(inside, "mode", far)
    g0 = gather_own(side, links, rims, inside)
    to_outer = lax.dynamic_slice_in_dim(jnp.concatenate([rims, x2a], axis=0), HALO * odd, HALO, axis=1)
    to_outer, g0 = lax.optimization_barrier((to_outer, g0))
    o02 = lax.ppermute(to_outer, "space", outer_pairs)
    x3a = lax.ppermute(x2a, "mode", near)
    x3b = lax.ppermute(x2b, "mode", near)
    o13 = lax.ppermute(o02, "mode", near)
    near_rims = jnp.concatenate([x1[:, :HALO], x1[:, OWN - HALO :]], axis=1)
    all_rims = jnp.concatenate([rims, x2a, near_rims, x3a], axis=0)
    inner = lax.ppermute(lax.dynamic_slice_in_dim(all_rims, HALO * (1 - odd), HALO, axis=1), "space", inner_pairs)
    table = coupling_table(me, pair_modes, pair_terms, pair_values)
    g1 = gather_own(side, links, x1)
    g2 = gather_own(side, links, x2a, x2b)
    g3 = gather_own(side, links, x3a, x3b)
    ha = gather_halo(side, links, o02, inner, 0)
    hb = gather_halo(side, links, o13, inner, 1)
    local, to_back, to_sibling = elements(side, (g0, g1, g2, g3), (ha, hb), table, elem_mats, links)
    back_outer = lax.ppermute(to_back, "space", outer_pairs)
    back_inner = lax.ppermute(to_sibling, "space", inner_pairs)
    own = scatter_own(side, local, links)
    return finish(side, own, back_outer, back_inner)


def solution(mesh):
    return jax.shard_map(
        body,
        mesh=mesh,
        in_specs=(P("mode", "space"), P(None, None, "space"), P(None, "space"), P(), P(), P()),
        out_specs=P("mode", "space"),
        check_vma=False,
    )
```

time: 75.3 us -> 80.2 us (1.065)
  the two profiles are of different devices: /device:TPU:6 before, /device:TPU:2 now
where the time goes in v3:
time: 80.2 us; the launch traced here: 79.9 us
  starting transfers between devices  26.6 us (33%)
  waiting for transfers between devices  26.3 us (33%)
  Pallas kernels  23.7 us (30%)
  local copies, waits for them, and re-layouts  2.69 us (3%)
    ppermute x1, waiting for transfers between devices, body(): x2a = lax.ppermute(rims, 'mode', far)  12.8 us
    pallas_call x4, Pallas kernels, gather_own(): pl.pallas_call(gather_whole_kernel if len(xs) == 1 else gather_parts_kern...  10.7 us
    ppermute x1, starting transfers between devices, body(): o02 = lax.ppermute(to_outer, 'space', outer_pairs)  10.1 us
    ppermute x1, starting transfers between devices, body(): back_outer = lax.ppermute(to_back, 'space', outer_pairs)  8.86 us
    ppermute x1, waiting for transfers between devices, body(): o02 = lax.ppermute(to_outer, 'space', outer_pairs)  6.89 us
    pallas_call x1, Pallas kernels, elements(): pl.pallas_call(element_kernel, out_shape=(jax.ShapeDtypeStruct((256, LANE...  4.85 us
    ppermute x1, waiting for transfers between devices, body(): x3a = lax.ppermute(x2a, 'mode', near)  4.32 us
    pallas_call x2, Pallas kernels, gather_halo(): pl.pallas_call(functools.partial(gather_halo_kernel, half), out_shape=jax...  3.73 us
  transfers between devices with their start and end apart: 10, of which 4 were waited for; matrix products, arithmetic and copies ran while one was open for 3% of the time, Pallas kernels for 20%

profile of v3, /device:TPU:2, one launch (start us, length us, event | category | flops | bytes accessed | tf_op | source)
XLA Modules:
  0.0 79.9 jit_solution(243225852202564646)
XLA Ops:
  0.0 1.9 %collective-permute-start.1 = (f32[30,3072]{1,0:T(8,128)}, f32[30,3072]{1,0:T(8,128)S(1)}, u32[]{:S(2)}, u32[]{:S(2)}) collective-permute-start(f32[30,3072]{1,0:T(8,128)} %param.6), channel_id=1, source_target_pairs={{0,64},{64,0},{128,192},{192,128},{1,65},{65,1},{129,193},{193,129... | collective-permute-start | bytes 1105928 | tf_op jit(solution)/shard_map/ppermute | solution.py:290
  1.9 1.0 %slice.17.inside_ref = f32[30,2048]{1,0:T(8,128)S(1)} slice(f32[30,3072]{1,0:T(8,128)} %param.6), slice={[0:30], [512:2560]} | slice | bytes 491520 | tf_op jit(solution)/shard_map/slice | solution.py:288
  3.0 3.4 %collective-permute-start.2 = (f32[30,2048]{1,0:T(8,128)S(1)}, f32[30,2048]{1,0:T(8,128)S(1)}, u32[]{:S(2)}, u32[]{:S(2)}) collective-permute-start(f32[30,2048]{1,0:T(8,128)S(1)} %slice.17.inside_ref), channel_id=1, source_target_pairs={{0,128},{64,192},{128,0},{192,64},{1,129},{65,193},{129,1},{193,65... | collective-permute-start | bytes 737288 | tf_op jit(solution)/shard_map/ppermute | solution.py:291
  6.3 0.9 %fusion.8 = (f32[30,512]{1,0:T(8,128)S(1)}, f32[30,512]{1,0:T(8,128)S(1)}) fusion(f32[30,3072]{1,0:T(8,128)} %param.6), kind=kLoop, calls=%fused_computation.18 | loop fusion | bytes 245760 | tf_op jit(solution)/shard_map/slice | solution.py:287
  7.2 0.1 collective-permute-start
  7.4 0.7 copy-done
  8.1 2.7 %shard_map.64.g0 = bf16[64,6144]{1,0:T(8,128)(2,1)S(1)} custom-call(s32[1]{0:T(128)} %bitcast.odd_ref, f32[30,1024]{1,0:T(8,128)S(1)} %pad_maximum_fusion.rims_ref, f32[30,2048]{1,0:T(8,128)S(1)} %slice.17.inside_ref, s32[6,1024]{1,0:T(8,128)S(1)} %copy-done), custom_call_target="tpu_custom_call" | custom-call | tf_op jit(solution)/shard_map/pallas_call | solution.py:137
  10.8 12.8 %collective-permute-done.rims_ref = f32[30,1024]{1,0:T(8,128)S(1)} collective-permute-done((f32[30,1024]{1,0:T(8,128)S(1)}, f32[30,1024]{1,0:T(8,128)S(1)}, u32[]{:S(2)}, u32[]{:S(2)}) %collective-permute-start) | collective-permute-done | bytes 122912 | tf_op jit(solution)/shard_map/ppermute | solution.py:289
  23.8 2.0 %collective-permute-start.4 = (f32[30,2048]{1,0:T(8,128)S(1)}, f32[30,2048]{1,0:T(8,128)S(1)}, u32[]{:S(2)}, u32[]{:S(2)}) collective-permute-start(f32[30,2048]{1,0:T(8,128)S(1)} %collective-permute-done.2.inside_ref), channel_id=1, source_target_pairs={{0,64},{64,0},{128,192},{192,128},{1,65},{65,1},{129,193},{193,129... | collective-permute-start | bytes 737288 | tf_op jit(solution)/shard_map/ppermute | solution.py:297
  25.9 4.3 %collective-permute-done.3.rims_ref = f32[30,1024]{1,0:T(8,128)S(1)} collective-permute-done((f32[30,1024]{1,0:T(8,128)S(1)}, f32[30,1024]{1,0:T(8,128)S(1)}, u32[]{:S(2)}, u32[]{:S(2)}) %collective-permute-start.3) | collective-permute-done | bytes 122912 | tf_op jit(solution)/shard_map/ppermute | solution.py:296
  30.2 0.2 fusion.3
  30.5 10.1 %collective-permute-start.5 = (f32[60,512]{1,0:T(8,128)S(1)}, f32[60,512]{1,0:T(8,128)S(1)}, u32[]{:S(2)}, u32[]{:S(2)}) collective-permute-start(f32[60,512]{1,0:T(8,128)S(1)} %fusion.6), channel_id=1, source_target_pairs={{1,2},{3,4},{5,6},{7,8},{9,10},{11,12},{13,14},{15,16},{17,18},{19... | collective-permute-start | bytes 368648 | tf_op jit(solution)/shard_map/ppermute | solution.py:295
  40.6 6.9 %collective-permute-done.5.outer_ref = f32[60,512]{1,0:T(8,128)S(1)} collective-permute-done((f32[60,512]{1,0:T(8,128)S(1)}, f32[60,512]{1,0:T(8,128)S(1)}, u32[]{:S(2)}, u32[]{:S(2)}) %collective-permute-start.5) | collective-permute-done | bytes 122912 | tf_op jit(solution)/shard_map/ppermute | solution.py:295
  47.5 1.0 %shard_map.70.table_ref = bf16[256,256]{1,0:T(8,128)(2,1)S(1)} custom-call(s32[1]{0:T(128)} %bitcast.1.me_ref, s32[2,1440]{1,0:T(2,128)S(1)} %copy-done.3, s32[1,1440]{1,0:T(1,128)S(1)} %reshape.14.terms_ref, f32[1,1440]{1,0:T(1,128)S(1)} %reshape.15.values_ref), custom_call_target="tpu_custom_call" | custom-call | tf_op jit(solution)/shard_map/pallas_call | solution.py:97
  48.5 2.7 %shard_map.66.g2 = bf16[64,6144]{1,0:T(8,128)(2,1)S(1)} custom-call(s32[1]{0:T(128)} %bitcast.odd_ref, f32[30,1024]{1,0:T(8,128)S(1)} %collective-permute-done.rims_ref, f32[30,2048]{1,0:T(8,128)S(1)} %collective-permute-done.2.inside_ref, s32[6,1024]{1,0:T(8,128)S(1)} %copy-done.1), custom_call_target="tpu_custom_call" | custom-call | tf_op jit(solution)/shard_map/pallas_call | solution.py:137
  51.2 2.7 %shard_map.65.g1 = bf16[64,6144]{1,0:T(8,128)(2,1)S(1)} custom-call(s32[1]{0:T(128)} %bitcast.odd_ref, f32[30,3072]{1,0:T(8,128)S(1)} %collective-permute-done.1.x_ref, s32[6,1024]{1,0:T(8,128)S(1)} %copy-done.1), custom_call_target="tpu_custom_call" | custom-call | tf_op jit(solution)/shard_map/pallas_call | solution.py:137
  53.9 2.7 %shard_map.67.g3 = bf16[64,6144]{1,0:T(8,128)(2,1)S(1)} custom-call(s32[1]{0:T(128)} %bitcast.odd_ref, f32[30,1024]{1,0:T(8,128)S(1)} %collective-permute-done.3.rims_ref, f32[30,2048]{1,0:T(8,128)S(1)} %collective-permute-done.4.inside_ref, s32[6,1024]{1,0:T(8,128)S(1)} %copy-done.1), custom_call_target="tpu_custom_call" | custom-call | tf_op jit(solution)/shard_map/pallas_call | solution.py:137
  56.6 1.9 %shard_map.68.ha = bf16[128,6144]{1,0:T(8,128)(2,1)S(1)} custom-call(s32[1]{0:T(128)} %bitcast.odd_ref, f32[60,512]{1,0:T(8,128)S(1)} %collective-permute-done.5.outer_ref, f32[120,512]{1,0:T(8,128)S(1)} %collective-permute-done.6.inner_ref, s32[6,1024]{1,0:T(8,128)S(1)} %copy-done.1), custom_call_target="tpu_custom_call" | custom-call | tf_op jit(solution)/shard_map/pallas_call | solution.py:165
  58.5 1.9 %shard_map.69.hb = bf16[128,6144]{1,0:T(8,128)(2,1)S(1)} custom-call(s32[1]{0:T(128)} %bitcast.odd_ref, f32[60,512]{1,0:T(8,128)S(1)} %collective-permute-done.7.outer_ref, f32[120,512]{1,0:T(8,128)S(1)} %collective-permute-done.6.inner_ref, s32[6,1024]{1,0:T(8,128)S(1)} %copy-done.1), custom_call_target="tpu_custom_call" | custom-call | tf_op jit(solution)/shard_map/pallas_call | solution.py:165
  60.4 4.8 %shard_map.71 = (bf16[256,6144]{1,0:T(8,128)(2,1)S(1)}, f32[30,512]{1,0:T(8,128)S(1)}, f32[30,512]{1,0:T(8,128)S(1)}) custom-call(s32[1]{0:T(128)} %bitcast.odd_ref, bf16[64,6144]{1,0:T(8,128)(2,1)S(1)} %shard_map.64.g0, bf16[64,6144]{1,0:T(8,128)(2,1)S(1)} %shard_map.65.g1, bf16[64,6144]{1,0:T(8,128)(2,1)S(1)} %shard_map.66.g2, ...), custom_call_target="tpu_custom_call" | custom-call | tf_op jit(solution)/shard_map/pallas_call | solution.py:229
  65.2 8.9 %collective-permute-start.8 = (f32[30,512]{1,0:T(8,128)S(1)}, f32[30,512]{1,0:T(8,128)S(1)}, u32[]{:S(2)}, u32[]{:S(2)}) collective-permute-start(f32[30,512]{1,0:T(8,128)S(1)} %get-tuple-element.13), channel_id=1, source_target_pairs={{1,2},{3,4},{5,6},{7,8},{9,10},{11,12},{13,14},{15,16},{17,18},{19... | collective-permute-start | bytes 184328 | tf_op jit(solution)/shard_map/ppermute | solution.py:309
  74.2 2.6 %shard_map.72.own_ref = f32[30,3072]{1,0:T(8,128)S(1)} custom-call(s32[1]{0:T(128)} %bitcast.odd_ref, bf16[256,6144]{1,0:T(8,128)(2,1)S(1)} %get-tuple-element.12.l_ref, s32[6,1024]{1,0:T(8,128)S(1)} %copy-done.1), custom_call_target="tpu_custom_call" | custom-call | tf_op jit(solution)/shard_map/pallas_call | solution.py:249
  76.8 2.3 %collective-permute-done.8.out_in_ref = f32[30,512]{1,0:T(8,128)S(1)} collective-permute-done((f32[30,512]{1,0:T(8,128)S(1)}, f32[30,512]{1,0:T(8,128)S(1)}, u32[]{:S(2)}, u32[]{:S(2)}) %collective-permute-start.8) | collective-permute-done | bytes 61472 | tf_op jit(solution)/shard_map/ppermute | solution.py:309
  79.1 0.8 shard_map.73
  (26 shorter events, 0.5 us)
Async XLA Ops:
  0.0 25.8 %collective-permute-start.1 = (f32[30,3072]{1,0:T(8,128)}, f32[30,3072]{1,0:T(8,128)S(1)}, u32[]{:S(2)}, u32[]{:S(2)}) collective-permute-start(f32[30,3072]{1,0:T(8,128)} %param.6), channel_id=1, source_target_pairs={{0,64},{64,0},{128,192},{192,128},{1,65},{65,1},{129,193},{193,129... | collective-permute-start | bytes 1105928 | tf_op jit(solution)/shard_map/ppermute | solution.py:290
  2.9 44.5 %copy-start.4 = (s32[1440]{0:T(1024)S(1)}, s32[1440]{0:T(1024)}, u32[]{:S(2)}) copy-start(s32[1440]{0:T(1024)} %param.10) | copy-start | bytes 17284
  2.9 44.5 %copy-start.5 = (f32[1440]{0:T(1024)S(1)}, f32[1440]{0:T(1024)}, u32[]{:S(2)}) copy-start(f32[1440]{0:T(1024)} %param.11) | copy-start | bytes 17284
  2.9 44.5 %copy-start.3 = (s32[2,1440]{1,0:T(2,128)S(1)}, s32[2,1440]{1,0:T(2,128)}, u32[]{:S(2)}) copy-start(s32[2,1440]{1,0:T(2,128)} %modes_ref.1) | copy-start | bytes 34564
  3.0 20.9 %collective-permute-start.2 = (f32[30,2048]{1,0:T(8,128)S(1)}, f32[30,2048]{1,0:T(8,128)S(1)}, u32[]{:S(2)}, u32[]{:S(2)}) collective-permute-start(f32[30,2048]{1,0:T(8,128)S(1)} %slice.17.inside_ref), channel_id=1, source_target_pairs={{0,128},{64,192},{128,0},{192,64},{1,129},{65,193},{129,1},{193,65... | collective-permute-start | bytes 737288 | tf_op jit(solution)/shard_map/ppermute | solution.py:291
  7.2 41.3 %copy-start.1 = (s32[6,1024]{1,0:T(8,128)S(1)}, s32[6,1024]{1,0:T(8,128)}, u32[]{:S(2)}) copy-start(s32[6,1024]{1,0:T(8,128)} %links_ref.15) | copy-start | bytes 73732
  7.2 16.4 %collective-permute-start = (f32[30,1024]{1,0:T(8,128)S(1)}, f32[30,1024]{1,0:T(8,128)S(1)}, u32[]{:S(2)}, u32[]{:S(2)}) collective-permute-start(f32[30,1024]{1,0:T(8,128)S(1)} %pad_maximum_fusion.rims_ref), channel_id=1, source_target_pairs={{0,128},{64,192},{128,0},{192,64},{1,129},{65,193},{129,1},{193,65... | collective-permute-start | bytes 368648 | tf_op jit(solution)/shard_map/ppermute | solution.py:289
  7.4 0.8 copy-start
  23.7 6.5 %collective-permute-start.3 = (f32[30,1024]{1,0:T(8,128)S(1)}, f32[30,1024]{1,0:T(8,128)S(1)}, u32[]{:S(2)}, u32[]{:S(2)}) collective-permute-start(f32[30,1024]{1,0:T(8,128)S(1)} %collective-permute-done.rims_ref), channel_id=1, source_target_pairs={{0,64},{64,0},{128,192},{192,128},{1,65},{65,1},{129,193},{193,129... | collective-permute-start | bytes 368648 | tf_op jit(solution)/shard_map/ppermute | solution.py:296
  23.8 30.0 %collective-permute-start.4 = (f32[30,2048]{1,0:T(8,128)S(1)}, f32[30,2048]{1,0:T(8,128)S(1)}, u32[]{:S(2)}, u32[]{:S(2)}) collective-permute-start(f32[30,2048]{1,0:T(8,128)S(1)} %collective-permute-done.2.inside_ref), channel_id=1, source_target_pairs={{0,64},{64,0},{128,192},{192,128},{1,65},{65,1},{129,193},{193,129... | collective-permute-start | bytes 737288 | tf_op jit(solution)/shard_map/ppermute | solution.py:297
  30.4 26.2 %collective-permute-start.6 = (f32[120,512]{1,0:T(8,128)S(1)}, f32[120,512]{1,0:T(8,128)S(1)}, u32[]{:S(2)}, u32[]{:S(2)}) collective-permute-start(f32[120,512]{1,0:T(8,128)S(1)} %fusion.3), channel_id=1, source_target_pairs={{0,1},{1,0},{2,3},{3,2},{4,5},{5,4},{6,7},{7,6},{8,9},{9,8},{10,11... | collective-permute-start | bytes 737288 | tf_op jit(solution)/shard_map/ppermute | solution.py:301
  30.5 17.0 %collective-permute-start.5 = (f32[60,512]{1,0:T(8,128)S(1)}, f32[60,512]{1,0:T(8,128)S(1)}, u32[]{:S(2)}, u32[]{:S(2)}) collective-permute-start(f32[60,512]{1,0:T(8,128)S(1)} %fusion.6), channel_id=1, source_target_pairs={{1,2},{3,4},{5,6},{7,8},{9,10},{11,12},{13,14},{15,16},{17,18},{19... | collective-permute-start | bytes 368648 | tf_op jit(solution)/shard_map/ppermute | solution.py:295
  47.4 11.0 %collective-permute-start.7 = (f32[60,512]{1,0:T(8,128)S(1)}, f32[60,512]{1,0:T(8,128)S(1)}, u32[]{:S(2)}, u32[]{:S(2)}) collective-permute-start(f32[60,512]{1,0:T(8,128)S(1)} %collective-permute-done.5.outer_ref), channel_id=1, source_target_pairs={{0,64},{64,0},{128,192},{192,128},{1,65},{65,1},{129,193},{193,129... | collective-permute-start | bytes 368648 | tf_op jit(solution)/shard_map/ppermute | solution.py:298
  56.6 3.8 %copy-start.2 = (f32[5,36,1024]{2,1,0:T(8,128)S(1)}, f32[5,36,1024]{2,1,0:T(8,128)}, u32[]{:S(2)}) copy-start(f32[5,36,1024]{2,1,0:T(8,128)} %mats_ref.1) | copy-start | bytes 2211844
  65.2 13.9 %collective-permute-start.8 = (f32[30,512]{1,0:T(8,128)S(1)}, f32[30,512]{1,0:T(8,128)S(1)}, u32[]{:S(2)}, u32[]{:S(2)}) collective-permute-start(f32[30,512]{1,0:T(8,128)S(1)} %get-tuple-element.13), channel_id=1, source_target_pairs={{1,2},{3,4},{5,6},{7,8},{9,10},{11,12},{13,14},{15,16},{17,18},{19... | collective-permute-start | bytes 184328 | tf_op jit(solution)/shard_map/ppermute | solution.py:309
  74.1 5.0 %collective-permute-start.9 = (f32[30,512]{1,0:T(8,128)S(1)}, f32[30,512]{1,0:T(8,128)S(1)}, u32[]{:S(2)}, u32[]{:S(2)}) collective-permute-start(f32[30,512]{1,0:T(8,128)S(1)} %get-tuple-element.14), channel_id=1, source_target_pairs={{0,1},{1,0},{2,3},{3,2},{4,5},{5,4},{6,7},{7,6},{8,9},{9,8},{10,11... | collective-permute-start | bytes 184328 | tf_op jit(solution)/shard_map/ppermute | solution.py:310

commit v4 on v3

--- a/solution.py
+++ b/solution.py
@@ -62,13 +62,14 @@
 
 def table_kernel(me_ref, modes_ref, terms_ref, values_ref, out_ref, ids_ref, v_ref):
     me = me_ref[0]
-    n = values_ref.shape[1]
+    n = values_ref.shape[0]
     wide = v_ref.shape[1]
     ids_ref[...] = jnp.full(ids_ref.shape, -1, jnp.int32)
     v_ref[...] = jnp.zeros(v_ref.shape, F32)
-    v_ref[0:1, 0:n] = values_ref[...]
+    v_ref[0, 0:n] = values_ref[...]
+    ids_ref[2, 0:n] = terms_ref[...]
     i_loc = modes_ref[0:1, :] - MD * me
-    ids_ref[0:1, 0:n] = jnp.where((i_loc >= 0) & (i_loc < MD), terms_ref[...] * 32 + i_loc, -1)
+    ids_ref[0:1, 0:n] = jnp.where((i_loc >= 0) & (i_loc < MD), ids_ref[2:3, 0:n] * 32 + i_loc, -1)
     j = modes_ref[1:2, :]
     part = (j >= MD).astype(jnp.int32) + (j >= 2 * MD).astype(jnp.int32) + (j >= 3 * MD).astype(jnp.int32)
     ids_ref[1:2, 0:n] = (part ^ me) * 64 + (j - MD * part)
@@ -101,7 +102,7 @@
         out_specs=VMEM,
         scratch_shapes=[pltpu.VMEM((8, wide), jnp.int32), pltpu.VMEM((8, wide), F32)],
         compiler_params=PARAMS,
-    )(me, pair_modes, pair_terms.reshape(1, n), pair_values.reshape(1, n))
+    )(me, pair_modes, pair_terms, pair_values)
 
 
 def gather_body(piece, odd_ref, links_ref, out_ref, t_ref):
@@ -189,10 +190,10 @@
             here = pl.ds(b * E + base, STEP)
             right = jnp.concatenate(
                 [
-                    g0[:, here] + ha[0:64, here],
-                    g1[:, here] + hb[0:64, here],
-                    g2[:, here] + ha[64:128, here],
-                    g3[:, here] + hb[64:128, here],
+                    g0[:, here] + hb[64:128, here],
+                    g1[:, here] + ha[64:128, here],
+                    g2[:, here] + hb[0:64, here],
+                    g3[:, here] + ha[0:64, here],
                 ],
                 axis=0,
             )
@@ -282,29 +283,30 @@
     inner_pairs = [(i, i ^ 1) for i in range(parts)]
     near = [(i, i ^ 1) for i in range(4)]
     far = [(i, i ^ 2) for i in range(4)]
+    cross = [(m * parts + i, (m ^ 3) * parts + j) for m in range(4) for i, j in outer_pairs]
     links = face_links
     side = odd.reshape(1)
     rims = jnp.concatenate([traces[:, :HALO], traces[:, OWN - HALO :]], axis=1)
     inside = traces[:, HALO : OWN - HALO]
     x2a = lax.ppermute(rims, "mode", far)
     x1 = lax.ppermute(traces, "mode", near)
-    x2b = lax.ppermute(inside, "mode", far)
     g0 = gather_own(side, links, rims, inside)
+    to_far, g0 = lax.optimization_barrier((inside, g0))
+    x2b = lax.ppermute(to_far, "mode", far)
     to_outer = lax.dynamic_slice_in_dim(jnp.concatenate([rims, x2a], axis=0), HALO * odd, HALO, axis=1)
-    to_outer, g0 = lax.optimization_barrier((to_outer, g0))
-    o02 = lax.ppermute(to_outer, "space", outer_pairs)
+    o31 = lax.ppermute(to_outer, ("mode", "space"), cross)
     x3a = lax.ppermute(x2a, "mode", near)
     x3b = lax.ppermute(x2b, "mode", near)
-    o13 = lax.ppermute(o02, "mode", near)
+    o20 = lax.ppermute(o31, "mode", near)
     near_rims = jnp.concatenate([x1[:, :HALO], x1[:, OWN - HALO :]], axis=1)
-    all_rims = jnp.concatenate([rims, x2a, near_rims, x3a], axis=0)
+    all_rims = jnp.concatenate([x3a, near_rims, x2a, rims], axis=0)
     inner = lax.ppermute(lax.dynamic_slice_in_dim(all_rims, HALO * (1 - odd), HALO, axis=1), "space", inner_pairs)
     table = coupling_table(me, pair_modes, pair_terms, pair_values)
     g1 = gather_own(side, links, x1)
     g2 = gather_own(side, links, x2a, x2b)
     g3 = gather_own(side, links, x3a, x3b)
-    ha = gather_halo(side, links, o02, inner, 0)
-    hb = gather_halo(side, links, o13, inner, 1)
+    ha = gather_halo(side, links, o31, inner, 0)
+    hb = gather_halo(side, links, o20, inner, 1)
     local, to_back, to_sibling = elements(side, (g0, g1, g2, g3), (ha, hb), table, elem_mats, links)
     back_outer = lax.ppermute(to_back, "space", outer_pairs)
     back_inner = lax.ppermute(to_sibling, "space", inner_pairs)

time: 80.2 us -> 82.1 us (1.024)
  the two profiles are of different devices: /device:TPU:2 before, /device:TPU:38 now
where the time goes in v4:
time: 82.1 us; the launch traced here: 81.8 us
  waiting for transfers between devices  28.5 us (35%)
  starting transfers between devices  26.4 us (32%)
  Pallas kernels  23.7 us (29%)
  local copies, waits for them, and re-layouts  2.68 us (3%)
    ppermute x1, waiting for transfers between devices, body(): x2a = lax.ppermute(rims, 'mode', far)  16.6 us
    pallas_call x4, Pallas kernels, gather_own(): pl.pallas_call(gather_whole_kernel if len(xs) == 1 else gather_parts_kern...  10.7 us
    ppermute x1, starting transfers between devices, body(): o31 = lax.ppermute(to_outer, ('mode', 'space'), cross)  9.93 us
    ppermute x1, starting transfers between devices, body(): back_outer = lax.ppermute(to_back, 'space', outer_pairs)  6.69 us
    pallas_call x1, Pallas kernels, elements(): pl.pallas_call(element_kernel, out_shape=(jax.ShapeDtypeStruct((256, LANE...  4.85 us
    ppermute x1, waiting for transfers between devices, body(): x3a = lax.ppermute(x2a, 'mode', near)  4.11 us
    ppermute x1, waiting for transfers between devices, body(): o31 = lax.ppermute(to_outer, ('mode', 'space'), cross)  3.93 us
    ppermute x1, waiting for transfers between devices, body(): back_outer = lax.ppermute(to_back, 'space', outer_pairs)  3.76 us
  transfers between devices with their start and end apart: 10, of which 4 were waited for; matrix products, arithmetic and copies ran while one was open for 3% of the time, Pallas kernels for 20%

profile of v4, /device:TPU:38, one launch (start us, length us, event | category | flops | bytes accessed | tf_op | source)
XLA Modules:
  0.0 81.8 jit_solution(4280827050083269917)
XLA Ops:
  0.0 0.1 collective-permute-start
  0.1 0.9 %fusion.8 = (f32[30,512]{1,0:T(8,128)S(1)}, f32[30,512]{1,0:T(8,128)S(1)}) fusion(f32[30,3072]{1,0:T(8,128)} %param.6), kind=kLoop, calls=%fused_computation.18 | loop fusion | bytes 245760 | tf_op jit(solution)/shard_map/slice | solution.py:289
  1.0 1.0 %slice.15.inside_ref = f32[30,2048]{1,0:T(8,128)S(1)} slice(f32[30,3072]{1,0:T(8,128)} %param.6), slice={[0:30], [512:2560]} | slice | bytes 491520 | tf_op jit(solution)/shard_map/slice | solution.py:290
  2.1 0.8 copy-done
  2.9 2.7 %shard_map.64.g0 = bf16[64,6144]{1,0:T(8,128)(2,1)S(1)} custom-call(s32[1]{0:T(128)} %bitcast.odd_ref, f32[30,1024]{1,0:T(8,128)S(1)} %pad_maximum_fusion.rims_ref, f32[30,2048]{1,0:T(8,128)S(1)} %slice.15.inside_ref, s32[6,1024]{1,0:T(8,128)S(1)} %copy-done), custom_call_target="tpu_custom_call" | custom-call | tf_op jit(solution)/shard_map/pallas_call | solution.py:138
  5.5 3.4 %collective-permute-start.2 = (f32[30,2048]{1,0:T(8,128)S(1)}, f32[30,2048]{1,0:T(8,128)S(1)}, u32[]{:S(2)}, u32[]{:S(2)}) collective-permute-start(f32[30,2048]{1,0:T(8,128)S(1)} %slice.15.inside_ref), channel_id=1, source_target_pairs={{0,128},{64,192},{128,0},{192,64},{1,129},{65,193},{129,1},{193,65... | collective-permute-start | bytes 737288 | tf_op jit(solution)/shard_map/ppermute | solution.py:295
  9.0 16.6 %collective-permute-done.1.rims_ref = f32[30,1024]{1,0:T(8,128)S(1)} collective-permute-done((f32[30,1024]{1,0:T(8,128)S(1)}, f32[30,1024]{1,0:T(8,128)S(1)}, u32[]{:S(2)}, u32[]{:S(2)}) %collective-permute-start.1) | collective-permute-done | bytes 122912 | tf_op jit(solution)/shard_map/ppermute | solution.py:291
  25.6 2.5 %collective-permute-start.3 = (f32[30,1024]{1,0:T(8,128)S(1)}, f32[30,1024]{1,0:T(8,128)S(1)}, u32[]{:S(2)}, u32[]{:S(2)}) collective-permute-start(f32[30,1024]{1,0:T(8,128)S(1)} %collective-permute-done.1.rims_ref), channel_id=1, source_target_pairs={{0,64},{64,0},{128,192},{192,128},{1,65},{65,1},{129,193},{193,129... | collective-permute-start | bytes 368648 | tf_op jit(solution)/shard_map/ppermute | solution.py:298
  28.4 4.1 %collective-permute-done.3.rims_ref = f32[30,1024]{1,0:T(8,128)S(1)} collective-permute-done((f32[30,1024]{1,0:T(8,128)S(1)}, f32[30,1024]{1,0:T(8,128)S(1)}, u32[]{:S(2)}, u32[]{:S(2)}) %collective-permute-start.3) | collective-permute-done | bytes 122912 | tf_op jit(solution)/shard_map/ppermute | solution.py:298
  32.5 0.2 fusion.2
  32.8 9.9 %collective-permute-start.5 = (f32[60,512]{1,0:T(8,128)S(1)}, f32[60,512]{1,0:T(8,128)S(1)}, u32[]{:S(2)}, u32[]{:S(2)}) collective-permute-start(f32[60,512]{1,0:T(8,128)S(1)} %fusion.6), channel_id=1, source_target_pairs={{1,194},{3,196},{5,198},{7,200},{9,202},{11,204},{13,206},{15,208}... | collective-permute-start | bytes 368648 | tf_op jit(solution)/shard_map/ppermute | solution.py:297
  42.7 3.9 %collective-permute-done.5.outer_ref = f32[60,512]{1,0:T(8,128)S(1)} collective-permute-done((f32[60,512]{1,0:T(8,128)S(1)}, f32[60,512]{1,0:T(8,128)S(1)}, u32[]{:S(2)}, u32[]{:S(2)}) %collective-permute-start.5) | collective-permute-done | bytes 122912 | tf_op jit(solution)/shard_map/ppermute | solution.py:297
  46.7 3.5 %collective-permute-start.7 = (f32[60,512]{1,0:T(8,128)S(1)}, f32[60,512]{1,0:T(8,128)S(1)}, u32[]{:S(2)}, u32[]{:S(2)}) collective-permute-start(f32[60,512]{1,0:T(8,128)S(1)} %collective-permute-done.5.outer_ref), channel_id=1, source_target_pairs={{0,64},{64,0},{128,192},{192,128},{1,65},{65,1},{129,193},{193,129... | collective-permute-start | bytes 368648 | tf_op jit(solution)/shard_map/ppermute | solution.py:300
  50.1 1.0 %shard_map.70.table_ref = bf16[256,256]{1,0:T(8,128)(2,1)S(1)} custom-call(s32[1]{0:T(128)} %bitcast.1.me_ref, s32[2,1440]{1,0:T(2,128)S(1)} %copy-done.3, s32[1440]{0:T(1024)S(1)} %copy-done.4, f32[1440]{0:T(1024)S(1)} %copy-done.5), custom_call_target="tpu_custom_call" | custom-call | tf_op jit(solution)/shard_map/pallas_call | solution.py:98
  51.1 2.7 %shard_map.66.g2 = bf16[64,6144]{1,0:T(8,128)(2,1)S(1)} custom-call(s32[1]{0:T(128)} %bitcast.odd_ref, f32[30,1024]{1,0:T(8,128)S(1)} %collective-permute-done.1.rims_ref, f32[30,2048]{1,0:T(8,128)S(1)} %collective-permute-done.2.inside_ref, s32[6,1024]{1,0:T(8,128)S(1)} %copy-done.1), custom_call_target="tpu_custom_call" | custom-call | tf_op jit(solution)/shard_map/pallas_call | solution.py:138
  53.8 2.7 %shard_map.65.g1 = bf16[64,6144]{1,0:T(8,128)(2,1)S(1)} custom-call(s32[1]{0:T(128)} %bitcast.odd_ref, f32[30,3072]{1,0:T(8,128)S(1)} %collective-permute-done.x_ref, s32[6,1024]{1,0:T(8,128)S(1)} %copy-done.1), custom_call_target="tpu_custom_call" | custom-call | tf_op jit(solution)/shard_map/pallas_call | solution.py:138
  56.5 2.7 %shard_map.67.g3 = bf16[64,6144]{1,0:T(8,128)(2,1)S(1)} custom-call(s32[1]{0:T(128)} %bitcast.odd_ref, f32[30,1024]{1,0:T(8,128)S(1)} %collective-permute-done.3.rims_ref, f32[30,2048]{1,0:T(8,128)S(1)} %collective-permute-done.4.inside_ref, s32[6,1024]{1,0:T(8,128)S(1)} %copy-done.1), custom_call_target="tpu_custom_call" | custom-call | tf_op jit(solution)/shard_map/pallas_call | solution.py:138
  59.2 1.9 %shard_map.68.ha = bf16[128,6144]{1,0:T(8,128)(2,1)S(1)} custom-call(s32[1]{0:T(128)} %bitcast.odd_ref, f32[60,512]{1,0:T(8,128)S(1)} %collective-permute-done.5.outer_ref, f32[120,512]{1,0:T(8,128)S(1)} %collective-permute-done.6.inner_ref, s32[6,1024]{1,0:T(8,128)S(1)} %copy-done.1), custom_call_target="tpu_custom_call" | custom-call | tf_op jit(solution)/shard_map/pallas_call | solution.py:166
  61.1 1.9 %shard_map.69.hb = bf16[128,6144]{1,0:T(8,128)(2,1)S(1)} custom-call(s32[1]{0:T(128)} %bitcast.odd_ref, f32[60,512]{1,0:T(8,128)S(1)} %collective-permute-done.7.outer_ref, f32[120,512]{1,0:T(8,128)S(1)} %collective-permute-done.6.inner_ref, s32[6,1024]{1,0:T(8,128)S(1)} %copy-done.1), custom_call_target="tpu_custom_call" | custom-call | tf_op jit(solution)/shard_map/pallas_call | solution.py:166
  63.0 4.8 %shard_map.71 = (bf16[256,6144]{1,0:T(8,128)(2,1)S(1)}, f32[30,512]{1,0:T(8,128)S(1)}, f32[30,512]{1,0:T(8,128)S(1)}) custom-call(s32[1]{0:T(128)} %bitcast.odd_ref, bf16[64,6144]{1,0:T(8,128)(2,1)S(1)} %shard_map.64.g0, bf16[64,6144]{1,0:T(8,128)(2,1)S(1)} %shard_map.65.g1, bf16[64,6144]{1,0:T(8,128)(2,1)S(1)} %shard_map.66.g2, ...), custom_call_target="tpu_custom_call" | custom-call | tf_op jit(solution)/shard_map/pallas_call | solution.py:230
  67.9 6.7 %collective-permute-start.8 = (f32[30,512]{1,0:T(8,128)S(1)}, f32[30,512]{1,0:T(8,128)S(1)}, u32[]{:S(2)}, u32[]{:S(2)}) collective-permute-start(f32[30,512]{1,0:T(8,128)S(1)} %get-tuple-element.13), channel_id=1, source_target_pairs={{1,2},{3,4},{5,6},{7,8},{9,10},{11,12},{13,14},{15,16},{17,18},{19... | collective-permute-start | bytes 184328 | tf_op jit(solution)/shard_map/ppermute | solution.py:311
  74.7 2.6 %shard_map.72.own_ref = f32[30,3072]{1,0:T(8,128)S(1)} custom-call(s32[1]{0:T(128)} %bitcast.odd_ref, bf16[256,6144]{1,0:T(8,128)(2,1)S(1)} %get-tuple-element.12.l_ref, s32[6,1024]{1,0:T(8,128)S(1)} %copy-done.1), custom_call_target="tpu_custom_call" | custom-call | tf_op jit(solution)/shard_map/pallas_call | solution.py:250
  77.3 3.8 %collective-permute-done.8.out_in_ref = f32[30,512]{1,0:T(8,128)S(1)} collective-permute-done((f32[30,512]{1,0:T(8,128)S(1)}, f32[30,512]{1,0:T(8,128)S(1)}, u32[]{:S(2)}, u32[]{:S(2)}) %collective-permute-start.8) | collective-permute-done | bytes 61472 | tf_op jit(solution)/shard_map/ppermute | solution.py:311
  81.1 0.8 shard_map.73
  (24 shorter events, 0.5 us)
Async XLA Ops:
  0.0 28.3 %collective-permute-start = (f32[30,3072]{1,0:T(8,128)}, f32[30,3072]{1,0:T(8,128)S(1)}, u32[]{:S(2)}, u32[]{:S(2)}) collective-permute-start(f32[30,3072]{1,0:T(8,128)} %param.6), channel_id=1, source_target_pairs={{0,64},{64,0},{128,192},{192,128},{1,65},{65,1},{129,193},{193,129... | collective-permute-start | bytes 1105928 | tf_op jit(solution)/shard_map/ppermute | solution.py:292
  2.0 48.1 %copy-start.3 = (s32[2,1440]{1,0:T(2,128)S(1)}, s32[2,1440]{1,0:T(2,128)}, u32[]{:S(2)}) copy-start(s32[2,1440]{1,0:T(2,128)} %modes_ref.1) | copy-start | bytes 34564
  2.0 48.1 %copy-start.4 = (s32[1440]{0:T(1024)S(1)}, s32[1440]{0:T(1024)}, u32[]{:S(2)}) copy-start(s32[1440]{0:T(1024)} %terms_ref.1) | copy-start | bytes 17284
  2.0 48.1 %copy-start.5 = (f32[1440]{0:T(1024)S(1)}, f32[1440]{0:T(1024)}, u32[]{:S(2)}) copy-start(f32[1440]{0:T(1024)} %values_ref.1) | copy-start | bytes 17284
  2.0 49.1 %copy-start.1 = (s32[6,1024]{1,0:T(8,128)S(1)}, s32[6,1024]{1,0:T(8,128)}, u32[]{:S(2)}) copy-start(s32[6,1024]{1,0:T(8,128)} %links_ref.15) | copy-start | bytes 73732
  2.1 0.8 copy-start
  5.5 22.7 %collective-permute-start.2 = (f32[30,2048]{1,0:T(8,128)S(1)}, f32[30,2048]{1,0:T(8,128)S(1)}, u32[]{:S(2)}, u32[]{:S(2)}) collective-permute-start(f32[30,2048]{1,0:T(8,128)S(1)} %slice.15.inside_ref), channel_id=1, source_target_pairs={{0,128},{64,192},{128,0},{192,64},{1,129},{65,193},{129,1},{193,65... | collective-permute-start | bytes 737288 | tf_op jit(solution)/shard_map/ppermute | solution.py:295
  8.9 16.7 %collective-permute-start.1 = (f32[30,1024]{1,0:T(8,128)S(1)}, f32[30,1024]{1,0:T(8,128)S(1)}, u32[]{:S(2)}, u32[]{:S(2)}) collective-permute-start(f32[30,1024]{1,0:T(8,128)S(1)} %pad_maximum_fusion.rims_ref), channel_id=1, source_target_pairs={{0,128},{64,192},{128,0},{192,64},{1,129},{65,193},{129,1},{193,65... | collective-permute-start | bytes 368648 | tf_op jit(solution)/shard_map/ppermute | solution.py:291
  25.6 6.8 %collective-permute-start.3 = (f32[30,1024]{1,0:T(8,128)S(1)}, f32[30,1024]{1,0:T(8,128)S(1)}, u32[]{:S(2)}, u32[]{:S(2)}) collective-permute-start(f32[30,1024]{1,0:T(8,128)S(1)} %collective-permute-done.1.rims_ref), channel_id=1, source_target_pairs={{0,64},{64,0},{128,192},{192,128},{1,65},{65,1},{129,193},{193,129... | collective-permute-start | bytes 368648 | tf_op jit(solution)/shard_map/ppermute | solution.py:298
  28.2 28.3 %collective-permute-start.4 = (f32[30,2048]{1,0:T(8,128)S(1)}, f32[30,2048]{1,0:T(8,128)S(1)}, u32[]{:S(2)}, u32[]{:S(2)}) collective-permute-start(f32[30,2048]{1,0:T(8,128)S(1)} %collective-permute-done.2.inside_ref), channel_id=1, source_target_pairs={{0,64},{64,0},{128,192},{192,128},{1,65},{65,1},{129,193},{193,129... | collective-permute-start | bytes 737288 | tf_op jit(solution)/shard_map/ppermute | solution.py:299
  32.7 26.5 %collective-permute-start.6 = (f32[120,512]{1,0:T(8,128)S(1)}, f32[120,512]{1,0:T(8,128)S(1)}, u32[]{:S(2)}, u32[]{:S(2)}) collective-permute-start(f32[120,512]{1,0:T(8,128)S(1)} %fusion.2), channel_id=1, source_target_pairs={{0,1},{1,0},{2,3},{3,2},{4,5},{5,4},{6,7},{7,6},{8,9},{9,8},{10,11... | collective-permute-start | bytes 737288 | tf_op jit(solution)/shard_map/ppermute | solution.py:303
  32.8 13.9 %collective-permute-start.5 = (f32[60,512]{1,0:T(8,128)S(1)}, f32[60,512]{1,0:T(8,128)S(1)}, u32[]{:S(2)}, u32[]{:S(2)}) collective-permute-start(f32[60,512]{1,0:T(8,128)S(1)} %fusion.6), channel_id=1, source_target_pairs={{1,194},{3,196},{5,198},{7,200},{9,202},{11,204},{13,206},{15,208}... | collective-permute-start | bytes 368648 | tf_op jit(solution)/shard_map/ppermute | solution.py:297
  46.7 14.4 %collective-permute-start.7 = (f32[60,512]{1,0:T(8,128)S(1)}, f32[60,512]{1,0:T(8,128)S(1)}, u32[]{:S(2)}, u32[]{:S(2)}) collective-permute-start(f32[60,512]{1,0:T(8,128)S(1)} %collective-permute-done.5.outer_ref), channel_id=1, source_target_pairs={{0,64},{64,0},{128,192},{192,128},{1,65},{65,1},{129,193},{193,129... | collective-permute-start | bytes 368648 | tf_op jit(solution)/shard_map/ppermute | solution.py:300
  59.2 3.8 %copy-start.2 = (f32[5,36,1024]{2,1,0:T(8,128)S(1)}, f32[5,36,1024]{2,1,0:T(8,128)}, u32[]{:S(2)}) copy-start(f32[5,36,1024]{2,1,0:T(8,128)} %mats_ref.1) | copy-start | bytes 2211844
  67.9 13.2 %collective-permute-start.8 = (f32[30,512]{1,0:T(8,128)S(1)}, f32[30,512]{1,0:T(8,128)S(1)}, u32[]{:S(2)}, u32[]{:S(2)}) collective-permute-start(f32[30,512]{1,0:T(8,128)S(1)} %get-tuple-element.13), channel_id=1, source_target_pairs={{1,2},{3,4},{5,6},{7,8},{9,10},{11,12},{13,14},{15,16},{17,18},{19... | collective-permute-start | bytes 184328 | tf_op jit(solution)/shard_map/ppermute | solution.py:311
  74.6 6.5 %collective-permute-start.9 = (f32[30,512]{1,0:T(8,128)S(1)}, f32[30,512]{1,0:T(8,128)S(1)}, u32[]{:S(2)}, u32[]{:S(2)}) collective-permute-start(f32[30,512]{1,0:T(8,128)S(1)} %get-tuple-element.14), channel_id=1, source_target_pairs={{0,1},{1,0},{2,3},{3,2},{4,5},{5,4},{6,7},{7,6},{8,9},{9,8},{10,11... | collective-permute-start | bytes 184328 | tf_op jit(solution)/shard_map/ppermute | solution.py:312

commit v5 on v4

--- a/solution.py
+++ b/solution.py
@@ -22,6 +22,7 @@
 STEP = 512
 VMEM = pl.BlockSpec(memory_space=pltpu.VMEM)
 PARAMS = pltpu.CompilerParams(vmem_limit_bytes=16 << 20)
+ELEMENT_PARAMS = pltpu.CompilerParams(vmem_limit_bytes=16 << 20)
 
 
 def split_hi_lo(x):
@@ -184,10 +185,10 @@
 
 
 def element_kernel(odd_ref, g0, g1, g2, g3, ha, hb, table_ref, mats_ref, links_ref, l_ref, outer_ref, inner_ref, y_ref):
-    def one(i, carry):
-        base = pl.multiple_of(i * STEP, STEP)
+    total = None
+    for base in range(0, E, STEP):
         for b in range(SLOTS):
-            here = pl.ds(b * E + base, STEP)
+            here = slice(b * E + base, b * E + base + STEP)
             right = jnp.concatenate(
                 [
                     g0[:, here] + hb[64:128, here],
@@ -201,24 +202,31 @@
             own = right[0:64].astype(F32)
             y_ref[b, 0:32] = own[0:32] + own[32:64]
             y_ref[b, 32:160] = got[0:128] + got[128:256]
-        for a in range(SLOTS):
-            acc = None
-            for b in range(SLOTS):
-                for k in range(TERMS + 1):
-                    m = mats_ref[k, 6 * a + b : 6 * a + b + 1, pl.ds(base, STEP)]
-                    term = m * y_ref[b, 32 * k : 32 * (k + 1)]
-                    acc = term if acc is None else acc + term
-            here = pl.ds(a * E + base, STEP)
-            _, quad, _ = codes(links_ref[a : a + 1, pl.ds(base, STEP)], odd_ref[0])
-            hi = acc.astype(BF16).astype(F32)
-            lo = acc - hi
-            for q in range(4):
-                l_ref[q * 64 : q * 64 + 32, here] = jnp.where(quad == q, hi, 0.0).astype(BF16)
-                l_ref[q * 64 + 32 : q * 64 + 64, here] = jnp.where(quad == q, lo, 0.0).astype(BF16)
-        return carry
-
-    lax.fori_loop(0, E // STEP, one, 0)
-    total = scatter_chunk(odd_ref, l_ref, links_ref, 3)
+        for first in range(0, SLOTS, 2):
+            slots = (first, first + 1)
+            for lane in range(0, STEP, 256):
+                here = slice(base + lane, base + lane + 256)
+                acc = [None, None]
+                for b in range(SLOTS):
+                    for k in range(TERMS + 1):
+                        y = y_ref[b, 32 * k : 32 * (k + 1), lane : lane + 256]
+                        for i, a in enumerate(slots):
+                            term = mats_ref[k, 6 * a + b : 6 * a + b + 1, here] * y
+                            acc[i] = term if acc[i] is None else acc[i] + term
+                for i, a in enumerate(slots):
+                    _, quad, _ = codes(links_ref[a : a + 1, here], odd_ref[0])
+                    hi = acc[i].astype(BF16).astype(F32)
+                    lo = acc[i] - hi
+                    there = slice(a * E + base + lane, a * E + base + lane + 256)
+                    for q in range(4):
+                        l_ref[q * 64 : q * 64 + 32, there] = jnp.where(quad == q, hi, 0.0).astype(BF16)
+                        l_ref[q * 64 + 32 : q * 64 + 64, there] = jnp.where(quad == q, lo, 0.0).astype(BF16)
+            for a in slots:
+                chunk_of, _, row = codes(links_ref[a : a + 1, base : base + STEP], odd_ref[0])
+                hot = one_hot(chunk_of, row, 3)
+                there = slice(a * E + base, a * E + base + STEP)
+                part = lax.dot_general(l_ref[:, there], hot, NT, preferred_element_type=F32)
+                total = part if total is None else total + part
     for q in range(4):
         both = total[q * 64 : q * 64 + 32] + total[q * 64 + 32 : q * 64 + 64]
         ref = inner_ref if q // 2 else outer_ref
@@ -233,7 +241,7 @@
         in_specs=[SMEM] + [VMEM] * 9,
         out_specs=(VMEM, VMEM, VMEM),
         scratch_shapes=[pltpu.VMEM((SLOTS, 160, STEP), F32)],
-        compiler_params=PARAMS,
+        compiler_params=ELEMENT_PARAMS,
     )(odd, *gs, *halos, table, mats, links)
 
 

time: 82.1 us -> 81.9 us (level)
  no operation moved by 1% of the time
where the time goes in v5:
time: 81.9 us; the launch traced here: 81.6 us
  waiting for transfers between devices  28.4 us (35%)
  starting transfers between devices  26.4 us (32%)
  Pallas kernels  23.5 us (29%)
  local copies, waits for them, and re-layouts  2.68 us (3%)
    ppermute x1, waiting for transfers between devices, body(): x2a = lax.ppermute(rims, 'mode', far)  16.6 us
    pallas_call x4, Pallas kernels, gather_own(): pl.pallas_call(gather_whole_kernel if len(xs) == 1 else gather_parts_kern...  10.7 us
    ppermute x1, starting transfers between devices, body(): o31 = lax.ppermute(to_outer, ('mode', 'space'), cross)  9.93 us
    ppermute x1, starting transfers between devices, body(): back_outer = lax.ppermute(to_back, 'space', outer_pairs)  6.69 us
    pallas_call x1, Pallas kernels, elements(): pl.pallas_call(element_kernel, out_shape=(jax.ShapeDtypeStruct((256, LANE...  4.6 us
    ppermute x1, waiting for transfers between devices, body(): x3a = lax.ppermute(x2a, 'mode', near)  4.11 us
    ppermute x1, waiting for transfers between devices, body(): o31 = lax.ppermute(to_outer, ('mode', 'space'), cross)  3.93 us
    ppermute x1, waiting for transfers between devices, body(): back_outer = lax.ppermute(to_back, 'space', outer_pairs)  3.75 us
  transfers between devices with their start and end apart: 10, of which 4 were waited for; matrix products, arithmetic and copies ran while one was open for 3% of the time, Pallas kernels for 20%

profile of v5, /device:TPU:38, one launch (start us, length us, event | category | flops | bytes accessed | tf_op | source)
XLA Modules:
  0.0 81.6 jit_solution(11096694966197219140)
XLA Ops:
  0.0 0.1 collective-permute-start
  0.1 0.9 %fusion.8 = (f32[30,512]{1,0:T(8,128)S(1)}, f32[30,512]{1,0:T(8,128)S(1)}) fusion(f32[30,3072]{1,0:T(8,128)} %param.6), kind=kLoop, calls=%fused_computation.18 | loop fusion | bytes 245760 | tf_op jit(solution)/shard_map/slice | solution.py:297
  1.0 1.0 %slice.15.inside_ref = f32[30,2048]{1,0:T(8,128)S(1)} slice(f32[30,3072]{1,0:T(8,128)} %param.6), slice={[0:30], [512:2560]} | slice | bytes 491520 | tf_op jit(solution)/shard_map/slice | solution.py:298
  2.1 0.8 copy-done
  2.9 2.7 %shard_map.64.g0 = bf16[64,6144]{1,0:T(8,128)(2,1)S(1)} custom-call(s32[1]{0:T(128)} %bitcast.odd_ref, f32[30,1024]{1,0:T(8,128)S(1)} %pad_maximum_fusion.rims_ref, f32[30,2048]{1,0:T(8,128)S(1)} %slice.15.inside_ref, s32[6,1024]{1,0:T(8,128)S(1)} %copy-done), custom_call_target="tpu_custom_call" | custom-call | tf_op jit(solution)/shard_map/pallas_call | solution.py:139
  5.5 3.4 %collective-permute-start.2 = (f32[30,2048]{1,0:T(8,128)S(1)}, f32[30,2048]{1,0:T(8,128)S(1)}, u32[]{:S(2)}, u32[]{:S(2)}) collective-permute-start(f32[30,2048]{1,0:T(8,128)S(1)} %slice.15.inside_ref), channel_id=1, source_target_pairs={{0,128},{64,192},{128,0},{192,64},{1,129},{65,193},{129,1},{193,65... | collective-permute-start | bytes 737288 | tf_op jit(solution)/shard_map/ppermute | solution.py:303
  9.0 16.6 %collective-permute-done.1.rims_ref = f32[30,1024]{1,0:T(8,128)S(1)} collective-permute-done((f32[30,1024]{1,0:T(8,128)S(1)}, f32[30,1024]{1,0:T(8,128)S(1)}, u32[]{:S(2)}, u32[]{:S(2)}) %collective-permute-start.1) | collective-permute-done | bytes 122912 | tf_op jit(solution)/shard_map/ppermute | solution.py:299
  25.6 2.5 %collective-permute-start.3 = (f32[30,1024]{1,0:T(8,128)S(1)}, f32[30,1024]{1,0:T(8,128)S(1)}, u32[]{:S(2)}, u32[]{:S(2)}) collective-permute-start(f32[30,1024]{1,0:T(8,128)S(1)} %collective-permute-done.1.rims_ref), channel_id=1, source_target_pairs={{0,64},{64,0},{128,192},{192,128},{1,65},{65,1},{129,193},{193,129... | collective-permute-start | bytes 368648 | tf_op jit(solution)/shard_map/ppermute | solution.py:306
  28.4 4.1 %collective-permute-done.3.rims_ref = f32[30,1024]{1,0:T(8,128)S(1)} collective-permute-done((f32[30,1024]{1,0:T(8,128)S(1)}, f32[30,1024]{1,0:T(8,128)S(1)}, u32[]{:S(2)}, u32[]{:S(2)}) %collective-permute-start.3) | collective-permute-done | bytes 122912 | tf_op jit(solution)/shard_map/ppermute | solution.py:306
  32.5 0.2 fusion.2
  32.8 9.9 %collective-permute-start.5 = (f32[60,512]{1,0:T(8,128)S(1)}, f32[60,512]{1,0:T(8,128)S(1)}, u32[]{:S(2)}, u32[]{:S(2)}) collective-permute-start(f32[60,512]{1,0:T(8,128)S(1)} %fusion.6), channel_id=1, source_target_pairs={{1,194},{3,196},{5,198},{7,200},{9,202},{11,204},{13,206},{15,208}... | collective-permute-start | bytes 368648 | tf_op jit(solution)/shard_map/ppermute | solution.py:305
  42.7 3.9 %collective-permute-done.5.outer_ref = f32[60,512]{1,0:T(8,128)S(1)} collective-permute-done((f32[60,512]{1,0:T(8,128)S(1)}, f32[60,512]{1,0:T(8,128)S(1)}, u32[]{:S(2)}, u32[]{:S(2)}) %collective-permute-start.5) | collective-permute-done | bytes 122912 | tf_op jit(solution)/shard_map/ppermute | solution.py:305
  46.7 3.5 %collective-permute-start.7 = (f32[60,512]{1,0:T(8,128)S(1)}, f32[60,512]{1,0:T(8,128)S(1)}, u32[]{:S(2)}, u32[]{:S(2)}) collective-permute-start(f32[60,512]{1,0:T(8,128)S(1)} %collective-permute-done.5.outer_ref), channel_id=1, source_target_pairs={{0,64},{64,0},{128,192},{192,128},{1,65},{65,1},{129,193},{193,129... | collective-permute-start | bytes 368648 | tf_op jit(solution)/shard_map/ppermute | solution.py:308
  50.1 1.0 %shard_map.70.table_ref = bf16[256,256]{1,0:T(8,128)(2,1)S(1)} custom-call(s32[1]{0:T(128)} %bitcast.1.me_ref, s32[2,1440]{1,0:T(2,128)S(1)} %copy-done.3, s32[1440]{0:T(1024)S(1)} %copy-done.4, f32[1440]{0:T(1024)S(1)} %copy-done.5), custom_call_target="tpu_custom_call" | custom-call | tf_op jit(solution)/shard_map/pallas_call | solution.py:99
  51.1 2.7 %shard_map.66.g2 = bf16[64,6144]{1,0:T(8,128)(2,1)S(1)} custom-call(s32[1]{0:T(128)} %bitcast.odd_ref, f32[30,1024]{1,0:T(8,128)S(1)} %collective-permute-done.1.rims_ref, f32[30,2048]{1,0:T(8,128)S(1)} %collective-permute-done.2.inside_ref, s32[6,1024]{1,0:T(8,128)S(1)} %copy-done.1), custom_call_target="tpu_custom_call" | custom-call | tf_op jit(solution)/shard_map/pallas_call | solution.py:139
  53.8 2.7 %shard_map.65.g1 = bf16[64,6144]{1,0:T(8,128)(2,1)S(1)} custom-call(s32[1]{0:T(128)} %bitcast.odd_ref, f32[30,3072]{1,0:T(8,128)S(1)} %collective-permute-done.x_ref, s32[6,1024]{1,0:T(8,128)S(1)} %copy-done.1), custom_call_target="tpu_custom_call" | custom-call | tf_op jit(solution)/shard_map/pallas_call | solution.py:139
  56.5 2.7 %shard_map.67.g3 = bf16[64,6144]{1,0:T(8,128)(2,1)S(1)} custom-call(s32[1]{0:T(128)} %bitcast.odd_ref, f32[30,1024]{1,0:T(8,128)S(1)} %collective-permute-done.3.rims_ref, f32[30,2048]{1,0:T(8,128)S(1)} %collective-permute-done.4.inside_ref, s32[6,1024]{1,0:T(8,128)S(1)} %copy-done.1), custom_call_target="tpu_custom_call" | custom-call | tf_op jit(solution)/shard_map/pallas_call | solution.py:139
  59.2 1.9 %shard_map.68.ha = bf16[128,6144]{1,0:T(8,128)(2,1)S(1)} custom-call(s32[1]{0:T(128)} %bitcast.odd_ref, f32[60,512]{1,0:T(8,128)S(1)} %collective-permute-done.5.outer_ref, f32[120,512]{1,0:T(8,128)S(1)} %collective-permute-done.6.inner_ref, s32[6,1024]{1,0:T(8,128)S(1)} %copy-done.1), custom_call_target="tpu_custom_call" | custom-call | tf_op jit(solution)/shard_map/pallas_call | solution.py:167
  61.1 1.9 %shard_map.69.hb = bf16[128,6144]{1,0:T(8,128)(2,1)S(1)} custom-call(s32[1]{0:T(128)} %bitcast.odd_ref, f32[60,512]{1,0:T(8,128)S(1)} %collective-permute-done.7.outer_ref, f32[120,512]{1,0:T(8,128)S(1)} %collective-permute-done.6.inner_ref, s32[6,1024]{1,0:T(8,128)S(1)} %copy-done.1), custom_call_target="tpu_custom_call" | custom-call | tf_op jit(solution)/shard_map/pallas_call | solution.py:167
  63.0 4.6 %shard_map.71 = (bf16[256,6144]{1,0:T(8,128)(2,1)S(1)}, f32[30,512]{1,0:T(8,128)S(1)}, f32[30,512]{1,0:T(8,128)S(1)}) custom-call(s32[1]{0:T(128)} %bitcast.odd_ref, bf16[64,6144]{1,0:T(8,128)(2,1)S(1)} %shard_map.64.g0, bf16[64,6144]{1,0:T(8,128)(2,1)S(1)} %shard_map.65.g1, bf16[64,6144]{1,0:T(8,128)(2,1)S(1)} %shard_map.66.g2, ...), custom_call_target="tpu_custom_call" | custom-call | tf_op jit(solution)/shard_map/pallas_call | solution.py:238
  67.6 6.7 %collective-permute-start.8 = (f32[30,512]{1,0:T(8,128)S(1)}, f32[30,512]{1,0:T(8,128)S(1)}, u32[]{:S(2)}, u32[]{:S(2)}) collective-permute-start(f32[30,512]{1,0:T(8,128)S(1)} %get-tuple-element.13), channel_id=1, source_target_pairs={{1,2},{3,4},{5,6},{7,8},{9,10},{11,12},{13,14},{15,16},{17,18},{19... | collective-permute-start | bytes 184328 | tf_op jit(solution)/shard_map/ppermute | solution.py:319
  74.4 2.6 %shard_map.72.own_ref = f32[30,3072]{1,0:T(8,128)S(1)} custom-call(s32[1]{0:T(128)} %bitcast.odd_ref, bf16[256,6144]{1,0:T(8,128)(2,1)S(1)} %get-tuple-element.12.l_ref, s32[6,1024]{1,0:T(8,128)S(1)} %copy-done.1), custom_call_target="tpu_custom_call" | custom-call | tf_op jit(solution)/shard_map/pallas_call | solution.py:258
  77.1 3.8 %collective-permute-done.8.out_in_ref = f32[30,512]{1,0:T(8,128)S(1)} collective-permute-done((f32[30,512]{1,0:T(8,128)S(1)}, f32[30,512]{1,0:T(8,128)S(1)}, u32[]{:S(2)}, u32[]{:S(2)}) %collective-permute-start.8) | collective-permute-done | bytes 61472 | tf_op jit(solution)/shard_map/ppermute | solution.py:319
  80.8 0.8 shard_map.73
  (24 shorter events, 0.5 us)
Async XLA Ops:
  0.0 28.3 %collective-permute-start = (f32[30,3072]{1,0:T(8,128)}, f32[30,3072]{1,0:T(8,128)S(1)}, u32[]{:S(2)}, u32[]{:S(2)}) collective-permute-start(f32[30,3072]{1,0:T(8,128)} %param.6), channel_id=1, source_target_pairs={{0,64},{64,0},{128,192},{192,128},{1,65},{65,1},{129,193},{193,129... | collective-permute-start | bytes 1105928 | tf_op jit(solution)/shard_map/ppermute | solution.py:300
  2.0 48.1 %copy-start.3 = (s32[2,1440]{1,0:T(2,128)S(1)}, s32[2,1440]{1,0:T(2,128)}, u32[]{:S(2)}) copy-start(s32[2,1440]{1,0:T(2,128)} %modes_ref.1) | copy-start | bytes 34564
  2.0 48.1 %copy-start.4 = (s32[1440]{0:T(1024)S(1)}, s32[1440]{0:T(1024)}, u32[]{:S(2)}) copy-start(s32[1440]{0:T(1024)} %terms_ref.1) | copy-start | bytes 17284
  2.0 48.1 %copy-start.5 = (f32[1440]{0:T(1024)S(1)}, f32[1440]{0:T(1024)}, u32[]{:S(2)}) copy-start(f32[1440]{0:T(1024)} %values_ref.1) | copy-start | bytes 17284
  2.0 49.1 %copy-start.1 = (s32[6,1024]{1,0:T(8,128)S(1)}, s32[6,1024]{1,0:T(8,128)}, u32[]{:S(2)}) copy-start(s32[6,1024]{1,0:T(8,128)} %links_ref.15) | copy-start | bytes 73732
  2.1 0.8 copy-start
  5.5 22.7 %collective-permute-start.2 = (f32[30,2048]{1,0:T(8,128)S(1)}, f32[30,2048]{1,0:T(8,128)S(1)}, u32[]{:S(2)}, u32[]{:S(2)}) collective-permute-start(f32[30,2048]{1,0:T(8,128)S(1)} %slice.15.inside_ref), channel_id=1, source_target_pairs={{0,128},{64,192},{128,0},{192,64},{1,129},{65,193},{129,1},{193,65... | collective-permute-start | bytes 737288 | tf_op jit(solution)/shard_map/ppermute | solution.py:303
  8.9 16.7 %collective-permute-start.1 = (f32[30,1024]{1,0:T(8,128)S(1)}, f32[30,1024]{1,0:T(8,128)S(1)}, u32[]{:S(2)}, u32[]{:S(2)}) collective-permute-start(f32[30,1024]{1,0:T(8,128)S(1)} %pad_maximum_fusion.rims_ref), channel_id=1, source_target_pairs={{0,128},{64,192},{128,0},{192,64},{1,129},{65,193},{129,1},{193,65... | collective-permute-start | bytes 368648 | tf_op jit(solution)/shard_map/ppermute | solution.py:299
  25.6 6.8 %collective-permute-start.3 = (f32[30,1024]{1,0:T(8,128)S(1)}, f32[30,1024]{1,0:T(8,128)S(1)}, u32[]{:S(2)}, u32[]{:S(2)}) collective-permute-start(f32[30,1024]{1,0:T(8,128)S(1)} %collective-permute-done.1.rims_ref), channel_id=1, source_target_pairs={{0,64},{64,0},{128,192},{192,128},{1,65},{65,1},{129,193},{193,129... | collective-permute-start | bytes 368648 | tf_op jit(solution)/shard_map/ppermute | solution.py:306
  28.2 28.3 %collective-permute-start.4 = (f32[30,2048]{1,0:T(8,128)S(1)}, f32[30,2048]{1,0:T(8,128)S(1)}, u32[]{:S(2)}, u32[]{:S(2)}) collective-permute-start(f32[30,2048]{1,0:T(8,128)S(1)} %collective-permute-done.2.inside_ref), channel_id=1, source_target_pairs={{0,64},{64,0},{128,192},{192,128},{1,65},{65,1},{129,193},{193,129... | collective-permute-start | bytes 737288 | tf_op jit(solution)/shard_map/ppermute | solution.py:307
  32.7 26.5 %collective-permute-start.6 = (f32[120,512]{1,0:T(8,128)S(1)}, f32[120,512]{1,0:T(8,128)S(1)}, u32[]{:S(2)}, u32[]{:S(2)}) collective-permute-start(f32[120,512]{1,0:T(8,128)S(1)} %fusion.2), channel_id=1, source_target_pairs={{0,1},{1,0},{2,3},{3,2},{4,5},{5,4},{6,7},{7,6},{8,9},{9,8},{10,11... | collective-permute-start | bytes 737288 | tf_op jit(solution)/shard_map/ppermute | solution.py:311
  32.8 13.9 %collective-permute-start.5 = (f32[60,512]{1,0:T(8,128)S(1)}, f32[60,512]{1,0:T(8,128)S(1)}, u32[]{:S(2)}, u32[]{:S(2)}) collective-permute-start(f32[60,512]{1,0:T(8,128)S(1)} %fusion.6), channel_id=1, source_target_pairs={{1,194},{3,196},{5,198},{7,200},{9,202},{11,204},{13,206},{15,208}... | collective-permute-start | bytes 368648 | tf_op jit(solution)/shard_map/ppermute | solution.py:305
  46.7 14.4 %collective-permute-start.7 = (f32[60,512]{1,0:T(8,128)S(1)}, f32[60,512]{1,0:T(8,128)S(1)}, u32[]{:S(2)}, u32[]{:S(2)}) collective-permute-start(f32[60,512]{1,0:T(8,128)S(1)} %collective-permute-done.5.outer_ref), channel_id=1, source_target_pairs={{0,64},{64,0},{128,192},{192,128},{1,65},{65,1},{129,193},{193,129... | collective-permute-start | bytes 368648 | tf_op jit(solution)/shard_map/ppermute | solution.py:308
  59.2 3.8 %copy-start.2 = (f32[5,36,1024]{2,1,0:T(8,128)S(1)}, f32[5,36,1024]{2,1,0:T(8,128)}, u32[]{:S(2)}) copy-start(f32[5,36,1024]{2,1,0:T(8,128)} %mats_ref.1) | copy-start | bytes 2211844
  67.6 13.2 %collective-permute-start.8 = (f32[30,512]{1,0:T(8,128)S(1)}, f32[30,512]{1,0:T(8,128)S(1)}, u32[]{:S(2)}, u32[]{:S(2)}) collective-permute-start(f32[30,512]{1,0:T(8,128)S(1)} %get-tuple-element.13), channel_id=1, source_target_pairs={{1,2},{3,4},{5,6},{7,8},{9,10},{11,12},{13,14},{15,16},{17,18},{19... | collective-permute-start | bytes 184328 | tf_op jit(solution)/shard_map/ppermute | solution.py:319
  74.3 6.5 %collective-permute-start.9 = (f32[30,512]{1,0:T(8,128)S(1)}, f32[30,512]{1,0:T(8,128)S(1)}, u32[]{:S(2)}, u32[]{:S(2)}) collective-permute-start(f32[30,512]{1,0:T(8,128)S(1)} %get-tuple-element.14), channel_id=1, source_target_pairs={{0,1},{1,0},{2,3},{3,2},{4,5},{5,4},{6,7},{7,6},{8,9},{9,8},{10,11... | collective-permute-start | bytes 184328 | tf_op jit(solution)/shard_map/ppermute | solution.py:320
